TPU v7x, 256 devices: a whole 4x4x8 slice. The times are simulated.
256 devices in a mesh: ctx: 32 (over y_lo, z, core), mp: 8 (over y_hi, x).
Axes of the slice: x: 4, y: 4 (y_hi: 2, y_lo: 2; y = y_hi * 2 + y_lo), z: 8, core: 2. Of those that a mesh axis runs over, the one named last changes fastest.
Arguments:
- tokens: bfloat16 [24576, 4096], P('ctx', 'mp'), may hold values from -20 to 20
- norm_gain: float32 [4096], P('mp'), may hold values from 0.5 to 1.5
- in_weight: bfloat16 [4096, 3, 4096], P('ctx', None, 'mp'), may hold values from -0.09375 to 0.09375
- short_weight: float32 [3, 3, 4096], P(None, None, 'mp'), may hold values from -3.5 to 3.5
- filters: bfloat16 [128, 256], P(None, 'mp'), may hold values from -0.5 to 0.5
- skip: float32 [4096], P('mp'), may hold values from -4 to 4
- out_weight: bfloat16 [4096, 4096], P('ctx', 'mp'), may hold values from -0.09375 to 0.09375
Outputs:
- block_out: bfloat16 [24576, 4096], P('ctx', 'mp')
All inputs are finite; a program needn't handle non-finite values.
Results may differ from a plain program's by a relative error of at most 0.022.
Values may be sent and summed in bfloat16 or wider, within the bound.
A program may use at most 64 MiB of HBM per device.

v0:
```python
import jax
import jax.numpy as jnp
from jax import lax
from jax.sharding import PartitionSpec as P

D = 4096
FILT = 128
SHORT = 3


epsilon = 1e-06


def short_filter(padded, weight):
    taps = weight.shape[0]
    span = padded.shape[0] - (taps - 1)
    total = jnp.zeros((span,) + padded.shape[1:], jnp.float32)
    for tap in range(taps):
        begin = taps - 1 - tap
        total = total + weight[tap] * padded[begin : begin + span].astype(jnp.float32)
    return total


def medium_filter(gated, filters, count):
    taps = filters.shape[0]
    groups = filters.shape[1]
    size = gated.shape[1] // groups
    grouped = gated.reshape(gated.shape[0], groups, size)
    extended = jnp.pad(grouped, ((0, 1), (0, 0), (0, 0)))
    blocks = count // taps
    first = extended[:count].reshape(blocks, taps, groups, size)
    second = extended[taps : count + taps].reshape(blocks, taps, groups, size)
    windows = jnp.concatenate([first, second], axis=1)
    row_idx = jnp.arange(taps, dtype=jnp.int32)[:, None]
    col_idx = jnp.arange(2 * taps, dtype=jnp.int32)[None, :]
    offset = row_idx + taps - 1 - col_idx
    onehot = (offset[:, :, None] == jnp.arange(taps, dtype=jnp.int32)[None, None, :]).astype(
        jnp.bfloat16
    )
    toeplitz = jnp.einsum(
        "rwi,ig->rwg", onehot, filters, preferred_element_type=jnp.float32
    ).astype(jnp.bfloat16)
    result = jnp.einsum("rwg,bwgk->brgk", toeplitz, windows, preferred_element_type=jnp.float32)
    return result.reshape(count, groups * size)


def hyena_mix(padded, short_weight, filters, skip, count):
    taps = filters.shape[0]
    shorted = short_filter(padded, short_weight)
    query = shorted[taps - 1 :, 0]
    gated = (shorted[:, 1] * shorted[:, 2]).astype(jnp.bfloat16)
    medium = medium_filter(gated, filters, count)
    direct = gated[taps - 1 :].astype(jnp.float32)
    return (query * (medium + skip * direct)).astype(jnp.bfloat16)


def body(tokens, norm_gain, in_weight, short_weight, filters, skip, out_weight):
    tok_count, width = tokens.shape
    token_f = tokens.astype(jnp.float32)
    squares = lax.psum(jnp.sum(token_f * token_f, axis=1), "mp")
    scale = lax.rsqrt(squares / D + epsilon)
    normed = (token_f * scale[:, None] * norm_gain).astype(jnp.bfloat16)
    full_rows = lax.all_gather(normed, "mp", axis=1, tiled=True)
    columns = full_rows
    streams = jnp.einsum(
        "tk,kqc->tqc",
        columns,
        lax.all_gather(in_weight, "ctx", axis=0, tiled=True),
        preferred_element_type=jnp.float32,
    ).astype(jnp.bfloat16)
    reach = FILT + SHORT - 2
    local_groups = filters.shape[1]
    group_size = width // local_groups
    ctx_count = lax.axis_size("ctx")
    per_device = local_groups // ctx_count
    spread = lax.all_to_all(
        streams.reshape(tok_count, 3, local_groups, group_size),
        "ctx",
        split_axis=2,
        concat_axis=0,
        tiled=True,
    )
    seq_total = tok_count * ctx_count
    my_index = lax.axis_index("ctx")
    chan_count = per_device * group_size
    my_short = lax.dynamic_slice_in_dim(short_weight, my_index * chan_count, chan_count, 2)
    my_filters = lax.dynamic_slice_in_dim(filters, my_index * per_device, per_device, 1)
    my_skip = lax.dynamic_slice_in_dim(skip, my_index * chan_count, chan_count, 0)
    padded = jnp.pad(spread.reshape(seq_total, 3, chan_count), ((reach, 0), (0, 0), (0, 0)))
    channel_mix = hyena_mix(padded, my_short, my_filters, my_skip, seq_total)
    channel_mix = channel_mix.reshape(seq_total, per_device, group_size)
    returned = lax.all_to_all(channel_mix, "ctx", split_axis=0, concat_axis=1, tiled=True)
    mixed = returned.reshape(tok_count, width)
    mixed_rows = lax.all_gather(mixed, "mp", axis=1, tiled=True)
    columns = mixed_rows
    branch = jnp.dot(
        columns,
        lax.all_gather(out_weight, "ctx", axis=0, tiled=True),
        preferred_element_type=jnp.float32,
    )
    return (token_f + branch).astype(jnp.bfloat16)


def solution(mesh):
    return jax.shard_map(
        body,
        mesh=mesh,
        in_specs=(
            P("ctx", "mp"),
            P("mp"),
            P("ctx", None, "mp"),
            P(None, None, "mp"),
            P(None, "mp"),
            P("mp"),
            P("ctx", "mp"),
        ),
        out_specs=P("ctx", "mp"),
        check_vma=False,
    )
```

profile of v0, /device:TPU:4, one launch (start us, length us, event | category | flops | bytes accessed | tf_op | source)
XLA Modules:
  0.0 535.9 jit_solution(10036401607072502809)
XLA Ops:
  6.5 1.4 fusion.8
  8.0 19.8 %psum.7 = f32[768]{0:T(1024)S(1)} all-reduce(f32[768]{0:T(1024)S(1)} %fusion.8), channel_id=1, replica_groups=mesh['ctx'=32,'mp'=8] {'mp'}, use_global_device_ids=true, to_apply=%region_1.0 | all-reduce | flops 768 | bytes 6144 | tf_op jit(solution)/shard_map/psum | solution.py:60
  27.7 2.3 fusion.10
  30.1 0.9 copy.23
  31.0 105.0 %all-gather.5.cloned.1.call-done = bf16[768,4096]{1,0:T(8,128)(2,1)} async-done(((bf16[768,512]{1,0:T(8,128)(2,1)}), bf16[768,4096]{1,0:T(8,128)(2,1)}) %all-gather.5.cloned.1.call-update) | async-done | bytes 6291472 | tf_op jit(solution)/shard_map/all_gather | solution.py:63
  136.0 108.3 %all-gather.7.cloned.1.call-done = bf16[4096,3,512]{0,2,1:T(8,128)(2,1)} async-done(((bf16[128,3,512]{0,2,1:T(8,128)(2,1)}), bf16[4096,3,512]{0,2,1:T(8,128)(2,1)}) %all-gather.7.cloned.1.call-update) | async-done | bytes 12582928 | tf_op jit(solution)/shard_map/all_gather | solution.py:68
  244.3 14.8 %fusion.4 = bf16[768,3,512]{0,2,1:T(8,128)(2,1)S(1)} fusion(bf16[4096,3,512]{0,2,1:T(8,128)(2,1)} %all-gather.7.cloned.1.call-done, bf16[768,4096]{1,0:T(8,128)(2,1)} %all-gather.5.cloned.1.call-done), kind=kOutput, calls=%fused_computation.9 | convolution fusion | flops 9664856064 | bytes 21233664 | tf_op jit(solution)/shard_map/tk,kqc->tqc/dot_general | solution.py:65
  259.1 1.6 copy.24
  260.7 6.4 %all-to-all-start = ((bf16[768,3,32,16]{0,3,1,2:T(8,128)(2,1)}), bf16[768,3,32,16]{0,3,1,2:T(8,128)(2,1)S(1)}, u32[]{:S(2)}, u32[]{:S(2)}) async-start(bf16[768,3,32,16]{0,3,1,2:T(8,128)(2,1)} %copy.24), calls=%async_computation | async-start | bytes 4718592 | tf_op jit(solution)/shard_map/all_to_all | solution.py:76
  267.1 0.7 all-gather.11.cloned.1.call-update
  267.8 0.2 all-gather.9.cloned.1.call-start
  268.1 0.8 dynamic_slice.11
  268.8 0.8 dynamic-slice_bitcast_fusion.2
  269.7 7.4 %fusion = bf16[1,128,256]{2,0,1:T(2,128)(2,1)S(1)} fusion(s32[128,256]{1,0:T(8,128)S(1)} %iota_subtract_fusion, bf16[128,32]{0,1:T(8,128)(2,1)S(1)} %copy-done, s32[]{:T(128)S(6)} %select_n.8), kind=kOutput, calls=%fused_computation.1 | convolution fusion | flops 12582912 | bytes 197124 | tf_op jit(solution)/shard_map/rwi,ig->rwg/dot_general | solution.py:40
  277.1 59.3 %all-to-all-done = bf16[768,3,32,16]{0,3,1,2:T(8,128)(2,1)S(1)} async-done(((bf16[768,3,32,16]{0,3,1,2:T(8,128)(2,1)}), bf16[768,3,32,16]{0,3,1,2:T(8,128)(2,1)S(1)}, u32[]{:S(2)}, u32[]{:S(2)}) %all-to-all-start) | async-done | bytes 2359328 | tf_op jit(solution)/shard_map/all_to_all | solution.py:76
  336.4 2.2 copy.25
  338.6 3.0 reshape.70
  341.6 2.1 multiply_add_fusion
  344.1 0.3 copy_bitcast_fusion
  344.4 0.6 fusion.17
  344.9 0.5 copy.28
  345.5 1.1 fusion.19
  346.5 0.5 broadcast.30
  347.1 1.2 reduce
  348.3 4.8 copy.46
  353.1 8.9 %reshape.83 = bf16[32,2,6144]{2,1,0:T(2,128)(2,1)S(1)} reshape(bf16[24576,16]{1,0:T(8,128)(2,1)} %copy.46) | data formatting | bytes 1572864
  362.0 27.4 %all_to_all.30 = bf16[32,2,6144]{2,1,0:T(2,128)(2,1)S(1)} all-to-all(bf16[32,2,6144]{2,1,0:T(2,128)(2,1)S(1)} %reshape.83), channel_id=1, replica_groups=mesh['ctx'=32,'mp'=8] {'ctx'}, dimensions={0} | all-to-all | bytes 1572864 | tf_op jit(solution)/shard_map/all_to_all | solution.py:92
  389.4 17.1 %reshape.84 = bf16[24576,1,16]{2,1,0:T(2,128)(2,1)} reshape(bf16[32,2,6144]{2,1,0:T(2,128)(2,1)S(1)} %all_to_all.30) | data formatting | bytes 1572864
  406.5 22.6 %copy.30 = bf16[24576,1,16]{0,2,1:T(8,128)(2,1)S(1)} copy(bf16[24576,1,16]{2,1,0:T(2,128)(2,1)} %reshape.84) | data formatting | bytes 1572864 | tf_op jit(solution)/shard_map/all_to_all | solution.py:92
  429.3 1.3 copy.31
  430.7 90.3 %all-gather.9.cloned.1.call-done = bf16[768,4096]{0,1:T(8,128)(2,1)} async-done(((bf16[768,512]{0,1:T(8,128)(2,1)}), bf16[768,4096]{0,1:T(8,128)(2,1)}) %all-gather.9.cloned.1.call-update) | async-done | bytes 6291472 | tf_op jit(solution)/shard_map/all_gather | solution.py:94
  521.0 8.3 %fusion.11 = bf16[768,512]{1,0:T(8,128)(2,1)} fusion(bf16[768,512]{1,0:T(8,128)(2,1)S(1)} %copy-done.2, bf16[768,4096]{0,1:T(8,128)(2,1)} %all-gather.9.cloned.1.call-done, bf16[4096,512]{1,0:T(8,128)(2,1)} %all-gather.11.cloned.1.call-done), kind=kOutput, calls=%fused_computation.15 | convolution fusion | flops 3222405120 | bytes 12058624 | tf_op jit(solution)/shard_map/dot_general | solution.py:96
  (21 shorter events, 0.8 us)
Async XLA Ops:
  6.5 263.2 %copy-start = (bf16[128,32]{0,1:T(8,128)(2,1)S(1)}, bf16[128,32]{0,1:T(8,128)(2,1)}, u32[]{:S(2)}) copy-start(bf16[128,32]{0,1:T(8,128)(2,1)} %param.11) | copy-start | bytes 24580
  6.5 23.5 %copy-start.3 = (bf16[128,3,512]{2,0,1:T(8,128)(2,1)S(1)}, bf16[128,3,512]{2,0,1:T(8,128)(2,1)}, u32[]{:S(2)}) copy-start(bf16[128,3,512]{2,0,1:T(8,128)(2,1)} %param.9) | copy-start | bytes 1179652
  6.5 129.5 %all-gather.5.cloned.1.call-start = ((), (), s32[]{:S(2)}) async-start(), calls=%async_computation.2 | async-start | bytes 7077888 | tf_op jit(solution)/shard_map/all_gather | solution.py:63
  30.0 214.3 %all-gather.7.cloned.1.call-start = ((), (), s32[]{:S(2)}) async-start(), calls=%async_computation.3 | async-start | bytes 12976128 | tf_op jit(solution)/shard_map/all_gather | solution.py:68
  260.7 75.7 %all-to-all-start = ((bf16[768,3,32,16]{0,3,1,2:T(8,128)(2,1)}), bf16[768,3,32,16]{0,3,1,2:T(8,128)(2,1)S(1)}, u32[]{:S(2)}, u32[]{:S(2)}) async-start(bf16[768,3,32,16]{0,3,1,2:T(8,128)(2,1)} %copy.24), calls=%async_computation | async-start | bytes 4718592 | tf_op jit(solution)/shard_map/all_to_all | solution.py:76
  267.1 163.6 %all-gather.11.cloned.1.call-start = ((), (), s32[]{:S(2)}) async-start(), calls=%async_computation.5 | async-start | bytes 4325376 | tf_op jit(solution)/shard_map/all_gather | solution.py:98
  267.8 253.2 %all-gather.9.cloned.1.call-start = ((), (), s32[]{:S(2)}) async-start(), calls=%async_computation.4 | async-start | bytes 7077888 | tf_op jit(solution)/shard_map/all_gather | solution.py:94
  429.1 91.9 %copy-start.2 = (bf16[768,512]{1,0:T(8,128)(2,1)S(1)}, bf16[768,512]{1,0:T(8,128)(2,1)}, u32[]{:S(2)}) copy-start(bf16[768,512]{1,0:T(8,128)(2,1)} %param.7) | copy-start | bytes 2359300
  521.0 8.3 %copy-start.1 = (bf16[128,32]{0,1:T(8,128)(2,1)S(1)}, bf16[128,32]{0,1:T(8,128)(2,1)}, u32[]{:S(2)}) copy-start(bf16[128,32]{0,1:T(8,128)(2,1)} %param.11) | copy-start | bytes 24580
Sparse Core Ops, SparseCore 0:
  30.2 105.8 all-gather.4
  137.8 106.4 all-gather.6
  269.8 86.9 all-gather.10
  430.8 90.2 all-gather.8
where the time goes:
time: 539 us; the launch traced here: 536 us
  waiting for transfers between devices  364 us (68%)
  local copies, waits for them, and re-layouts  65.6 us (12%)
  blocking collectives  47.2 us (9%)
  matrix products  31.1 us (6%)
  between operations  13.3 us (2%)
  other arithmetic  8.32 us (2%)
  starting transfers between devices  6.71 us (1%)
    all_gather x1, waiting for transfers between devices, body(): lax.all_gather(in_weight, 'ctx', axis=0, tiled=True)  108 us
    all_gather x1, waiting for transfers between devices, body(): full_rows = lax.all_gather(normed, 'mp', axis=1, tiled=True)  105 us
    all_gather x1, waiting for transfers between devices, body(): mixed_rows = lax.all_gather(mixed, 'mp', axis=1, tiled=True)  90.3 us
    all_to_all x1, waiting for transfers between devices, body(): lax.all_to_all(streams.reshape(tok_count, 3, local_groups, group_size), '...  59.3 us
    unnamed x14, local copies, waits for them, and re-layouts  32.1 us
    all_to_all x1, blocking collectives, body(): lax.all_to_all(channel_mix, 'ctx', split_axis=0, concat_axis=1, tiled=True)  27.4 us
    all_to_all x2, local copies, waits for them, and re-layouts, body(): lax.all_to_all(channel_mix, 'ctx', split_axis=0, concat_axis=1, tiled=True)  23.9 us
    psum x1, blocking collectives, body(): squares = lax.psum(jnp.sum(token_f * token_f, axis=1), 'mp')  19.8 us
  transfers between devices with their start and end apart: 5, of which 4 were waited for; matrix products, arithmetic and copies ran while one was open for 14% of the time, Pallas kernels for 0%

commit v1 on v0

--- a/solution.py
+++ b/solution.py
@@ -56,49 +56,32 @@
 
 def body(tokens, norm_gain, in_weight, short_weight, filters, skip, out_weight):
     tok_count, width = tokens.shape
-    token_f = tokens.astype(jnp.float32)
-    squares = lax.psum(jnp.sum(token_f * token_f, axis=1), "mp")
+    rows = lax.all_gather(tokens, "mp", axis=1, tiled=True)
+    gain = lax.all_gather(norm_gain, "mp", axis=0, tiled=True)
+    rows_f = rows.astype(jnp.float32)
+    squares = jnp.sum(rows_f * rows_f, axis=1)
     scale = lax.rsqrt(squares / D + epsilon)
-    normed = (token_f * scale[:, None] * norm_gain).astype(jnp.bfloat16)
-    full_rows = lax.all_gather(normed, "mp", axis=1, tiled=True)
-    columns = full_rows
+    normed = (rows_f * scale[:, None] * gain).astype(jnp.bfloat16)
     streams = jnp.einsum(
-        "tk,kqc->tqc",
-        columns,
-        lax.all_gather(in_weight, "ctx", axis=0, tiled=True),
+        "tk,qkc->tqc",
+        normed,
+        lax.all_gather(jnp.transpose(in_weight, (1, 0, 2)), "ctx", axis=1, tiled=True),
         preferred_element_type=jnp.float32,
     ).astype(jnp.bfloat16)
     reach = FILT + SHORT - 2
-    local_groups = filters.shape[1]
-    group_size = width // local_groups
     ctx_count = lax.axis_size("ctx")
-    per_device = local_groups // ctx_count
-    spread = lax.all_to_all(
-        streams.reshape(tok_count, 3, local_groups, group_size),
-        "ctx",
-        split_axis=2,
-        concat_axis=0,
-        tiled=True,
+    halo = lax.ppermute(
+        streams[tok_count - reach :], "ctx", [(i, i + 1) for i in range(ctx_count - 1)]
     )
-    seq_total = tok_count * ctx_count
-    my_index = lax.axis_index("ctx")
-    chan_count = per_device * group_size
-    my_short = lax.dynamic_slice_in_dim(short_weight, my_index * chan_count, chan_count, 2)
-    my_filters = lax.dynamic_slice_in_dim(filters, my_index * per_device, per_device, 1)
-    my_skip = lax.dynamic_slice_in_dim(skip, my_index * chan_count, chan_count, 0)
-    padded = jnp.pad(spread.reshape(seq_total, 3, chan_count), ((reach, 0), (0, 0), (0, 0)))
-    channel_mix = hyena_mix(padded, my_short, my_filters, my_skip, seq_total)
-    channel_mix = channel_mix.reshape(seq_total, per_device, group_size)
-    returned = lax.all_to_all(channel_mix, "ctx", split_axis=0, concat_axis=1, tiled=True)
-    mixed = returned.reshape(tok_count, width)
+    padded = jnp.concatenate([halo, streams], axis=0)
+    mixed = hyena_mix(padded, short_weight, filters, skip, tok_count)
     mixed_rows = lax.all_gather(mixed, "mp", axis=1, tiled=True)
-    columns = mixed_rows
     branch = jnp.dot(
-        columns,
+        mixed_rows,
         lax.all_gather(out_weight, "ctx", axis=0, tiled=True),
         preferred_element_type=jnp.float32,
     )
-    return (token_f + branch).astype(jnp.bfloat16)
+    return (tokens.astype(jnp.float32) + branch).astype(jnp.bfloat16)
 
 
 def solution(mesh):

time: 539 us -> 389 us (0.72)
  waiting for transfers between devices: 364 us -> 289 us
  local copies, waits for them, and re-layouts: 65.6 us -> 9.2 us
  blocking collectives: 47.2 us -> 28.4 us
    all_to_all x1 -> x0, waiting for transfers between devices: 59.3 us -> none  [body(): lax.all_to_all(streams.reshape(tok_count, 3, local_groups, group_size), '...]
    all_gather x2, waiting for transfers between devices: 213 us -> 157 us  [the longest x1 78.5 us: body(): rows = lax.all_gather(tokens, 'mp', axis=1, tiled=True)]
    unnamed x14 -> x11, local copies, waits for them, and re-layouts: 32.1 us -> 2.78 us
    all_gather x0 -> x1, blocking collectives: none -> 28.4 us  [body(): gain = lax.all_gather(norm_gain, 'mp', axis=0, tiled=True)]
    all_to_all x1 -> x0, blocking collectives: 27.4 us -> none  [body(): lax.all_to_all(channel_mix, 'ctx', split_axis=0, concat_axis=1, tiled=True)]
    all_to_all x3 -> x0, local copies, waits for them, and re-layouts: 26.1 us -> none  [the longest x2 23.9 us: body(): lax.all_to_all(channel_mix, 'ctx', split_axis=0, concat_axis=1, tiled=True)]
    all_gather x1, waiting for transfers between devices: 0.02 us -> 25.2 us  [body(): lax.all_gather(out_weight, 'ctx', axis=0, tiled=True)]
    psum x1 -> x0, blocking collectives: 19.8 us -> none  [body(): squares = lax.psum(jnp.sum(token_f * token_f, axis=1), 'mp')]
  transfers between devices with their start and end apart: 5 -> 5, of which waited for: 4 -> 4; matrix products, arithmetic and copies ran while one was open for 14% -> 11% of each run, Pallas kernels for 0% -> 0%
where the time goes in v1:
time: 389 us; the launch traced here: 387 us
  waiting for transfers between devices  289 us (74%)
  matrix products  34.9 us (9%)
  blocking collectives  28.4 us (7%)
  between operations  13.3 us (3%)
  other arithmetic  9.79 us (3%)
  local copies, waits for them, and re-layouts  9.2 us (2%)
    all_gather x1, waiting for transfers between devices, body(): mixed_rows = lax.all_gather(mixed, 'mp', axis=1, tiled=True)  105 us
    all_gather x1, waiting for transfers between devices, body(): rows = lax.all_gather(tokens, 'mp', axis=1, tiled=True)  78.5 us
    all_gather x1, waiting for transfers between devices, body(): lax.all_gather(jnp.transpose(in_weight, (1, 0, 2)), 'ctx', axis=1, tiled=...  78.2 us
    all_gather x1, blocking collectives, body(): gain = lax.all_gather(norm_gain, 'mp', axis=0, tiled=True)  28.4 us
    all_gather x1, waiting for transfers between devices, body(): lax.all_gather(out_weight, 'ctx', axis=0, tiled=True)  25.2 us
    dot_general x1, matrix products, body(): jnp.einsum('tk,qkc->tqc', normed, lax.all_gather(jnp.transpose(in_weight,...  14.9 us
    dot_general x1, matrix products, medium_filter(): jnp.einsum('rwi,ig->rwg', onehot, filters, preferred_element_type=jnp.flo...  8.73 us
    dot_general x1, matrix products, body(): jnp.dot(mixed_rows, lax.all_gather(out_weight, 'ctx', axis=0, tiled=True)...  8.3 us
  transfers between devices with their start and end apart: 5, of which 4 were waited for; matrix products, arithmetic and copies ran while one was open for 11% of the time, Pallas kernels for 0%

profile of v1, /device:TPU:4, one launch (start us, length us, event | category | flops | bytes accessed | tf_op | source)
XLA Modules:
  0.0 387.2 jit_solution(3419213746029134804)
XLA Ops:
  6.5 0.7 all-gather.6.cloned.1.call-update
  7.3 0.0 all-gather.8.cloned.1.call-start
  7.3 0.7 all-gather.8.cloned.1.call-update
  8.0 0.0 all-gather.12.cloned.1.call-start
  8.1 0.7 all-gather.12.cloned.1.call-update
  8.7 0.0 all-gather.10.cloned.1.call-start
  8.8 28.4 %all-gather = f32[8,1,512]{2,1,0:T(1,128)S(1)} all-gather(f32[1,1,512]{2,1,0:T(1,128)} %bitcast.55), channel_id=1, replica_groups=mesh['ctx'=32,'mp'=8] {'mp'}, dimensions={0}, use_global_device_ids=true | all-gather | bytes 18432 | tf_op jit(solution)/shard_map/all_gather | solution.py:60
  37.2 0.1 iota_subtract_fusion
  37.3 78.5 %all-gather.6.cloned.1.call-done = bf16[768,4096]{1,0:T(8,128)(2,1)} async-done(((bf16[768,512]{1,0:T(8,128)(2,1)}), bf16[768,4096]{1,0:T(8,128)(2,1)}) %all-gather.6.cloned.1.call-update) | async-done | bytes 6291472 | tf_op jit(solution)/shard_map/all_gather | solution.py:59
  115.8 4.1 %fusion.1 = f32[768]{0:T(1024)S(1)} fusion(bf16[768,4096]{1,0:T(8,128)(2,1)} %all-gather.6.cloned.1.call-done), kind=kLoop, calls=%fused_computation.4 | loop fusion | flops 9436416 | bytes 6294528 | tf_op jit(solution)/shard_map/reduce_sum | solution.py:62
  119.9 78.2 %all-gather.8.cloned.1.call-done = bf16[3,4096,512]{2,1,0:T(8,128)(2,1)} async-done(((bf16[3,128,512]{2,1,0:T(8,128)(2,1)}), bf16[3,4096,512]{2,1,0:T(8,128)(2,1)}) %all-gather.8.cloned.1.call-update) | async-done | bytes 12582928 | tf_op jit(solution)/shard_map/all_gather | solution.py:68
  198.1 14.9 %fusion.14 = bf16[768,3,512]{2,0,1:T(8,128)(2,1)S(1)} fusion(bf16[3,4096,512]{2,1,0:T(8,128)(2,1)} %all-gather.8.cloned.1.call-done, bf16[768,4096]{1,0:T(8,128)(2,1)} %all-gather.6.cloned.1.call-done, f32[4096]{0:T(1024)S(1)} %bitcast.54, f32[768]{0:T(1024)S(1)} %add_rsqrt_fusion), kind=kOutput, calls=%fused_computation.21 | convolution fusion | flops 9677438976 | bytes 21253120 | tf_op jit(solution)/shard_map/tk,qkc->tqc/dot_general | solution.py:65
  213.0 0.1 slice.55
  213.1 2.4 collective-permute-start
  215.5 8.7 %convert_bitcast_fusion = bf16[128,256,32,1]{1,2,0,3:T(8,128)(2,1)} fusion(s32[128,256]{1,0:T(8,128)S(1)} %iota_subtract_fusion, bf16[128,32]{0,1:T(8,128)(2,1)S(1)} %copy-done), kind=kOutput, calls=%fused_computation.20 | convolution fusion | flops 273678336 | bytes 2236416 | tf_op jit(solution)/shard_map/rwi,ig->rwg/dot_general | solution.py:40
  224.2 2.0 multiply_add_fusion
  226.3 2.4 copy-done.1
  228.7 0.3 fusion.17
  229.0 0.1 slice.63
  229.1 0.6 copy.17
  229.7 1.2 copy.16
  230.8 2.0 reshape.54
  232.8 0.1 copy.18
  232.9 0.1 copy_bitcast_fusion.1
  233.1 2.9 fusion.24
  236.0 0.6 copy.21
  236.7 0.4 copy.34
  237.0 1.7 copy.22
  238.7 3.3 fusion.19
  242.0 25.2 %all-gather.12.cloned.1.call-done = bf16[4096,512]{1,0:T(8,128)(2,1)} async-done(((bf16[128,512]{1,0:T(8,128)(2,1)}), bf16[4096,512]{1,0:T(8,128)(2,1)}) %all-gather.12.cloned.1.call-update) | async-done | bytes 4194320 | tf_op jit(solution)/shard_map/all_gather | solution.py:81
  267.1 105.2 %all-gather.10.cloned.1.call-done = bf16[768,4096]{1,0:T(8,128)(2,1)} async-done(((bf16[768,512]{1,0:T(8,128)(2,1)}), bf16[768,4096]{1,0:T(8,128)(2,1)}) %all-gather.10.cloned.1.call-update) | async-done | bytes 6291472 | tf_op jit(solution)/shard_map/all_gather | solution.py:78
  372.4 8.3 %add_convert_fusion = bf16[768,512]{1,0:T(8,128)(2,1)} fusion(bf16[768,512]{1,0:T(8,128)(2,1)S(1)} %copy-done.2, bf16[768,4096]{1,0:T(8,128)(2,1)} %all-gather.10.cloned.1.call-done, bf16[4096,512]{1,0:T(8,128)(2,1)} %all-gather.12.cloned.1.call-done), kind=kOutput, calls=%fused_computation.33 | convolution fusion | flops 3222405120 | bytes 12058624 | tf_op jit(solution)/shard_map/dot_general | solution.py:79
  (15 shorter events, 0.1 us)
Async XLA Ops:
  6.5 208.9 %copy-start = (bf16[128,32]{0,1:T(8,128)(2,1)S(1)}, bf16[128,32]{0,1:T(8,128)(2,1)}, u32[]{:S(2)}) copy-start(bf16[128,32]{0,1:T(8,128)(2,1)} %param.11) | copy-start | bytes 24580
  6.5 109.3 %all-gather.6.cloned.1.call-start = ((), (), s32[]{:S(2)}) async-start(), calls=%async_computation | async-start | bytes 7077888 | tf_op jit(solution)/shard_map/all_gather | solution.py:59
  7.3 190.8 %all-gather.8.cloned.1.call-start = ((), (), s32[]{:S(2)}) async-start(), calls=%async_computation.1 | async-start | bytes 12976128 | tf_op jit(solution)/shard_map/all_gather | solution.py:68
  8.0 259.1 %all-gather.12.cloned.1.call-start = ((), (), s32[]{:S(2)}) async-start(), calls=%async_computation.3 | async-start | bytes 4325376 | tf_op jit(solution)/shard_map/all_gather | solution.py:81
  8.7 363.6 %all-gather.10.cloned.1.call-start = ((), (), s32[]{:S(2)}) async-start(), calls=%async_computation.2 | async-start | bytes 7077888 | tf_op jit(solution)/shard_map/all_gather | solution.py:78
  198.1 17.4 %copy-start.3 = (f32[3,3,512]{2,1,0:T(4,128)S(1)}, f32[3,3,512]{2,1,0:T(4,128)}, u32[]{:S(2)}) copy-start(f32[3,3,512]{2,1,0:T(4,128)} %param.10) | copy-start | bytes 55300
  213.1 11.1 %collective-permute-start = (bf16[129,3,512]{2,0,1:T(8,128)(2,1)S(1)}, bf16[129,3,512]{2,0,1:T(8,128)(2,1)S(1)}, u32[]{:S(2)}, u32[]{:S(2)}) collective-permute-start(bf16[129,3,512]{2,0,1:T(8,128)(2,1)S(1)} %slice.55), channel_id=1, source_target_pairs={{0,8},{8,16},{16,24},{24,32},{32,40},{40,48},{48,56},{56,64},{64,7... | collective-permute-start | bytes 1188872 | tf_op jit(solution)/shard_map/ppermute | solution.py:73
  226.3 2.4 copy-start.1
  236.6 2.0 copy-start.4
  237.0 135.4 %copy-start.2 = (bf16[768,512]{1,0:T(8,128)(2,1)S(1)}, bf16[768,512]{1,0:T(8,128)(2,1)}, u32[]{:S(2)}) copy-start(bf16[768,512]{1,0:T(8,128)(2,1)} %param.7) | copy-start | bytes 2359300
Sparse Core Ops, SparseCore 0:
  9.8 105.9 all-gather.5
  117.7 80.3 all-gather.7
  199.9 67.1 all-gather.11
  269.5 102.8 all-gather.9

commit v2 on v1

v2 whole, which is shorter than its diff:
```python
import jax
import jax.numpy as jnp
from jax import lax
from jax.experimental import pallas as pl
from jax.experimental.pallas import tpu as pltpu
from jax.sharding import PartitionSpec as P

D = 4096
EPS = 1e-06
NX, NZ, NY = 4, 8, 2
ROWS, COLS, DEPTH = 768, 512, 128
BLK = 128
NB = ROWS // BLK
XROWS = ROWS + 16
HALF = 384
GSIZE = 16
BF = jnp.bfloat16
F32 = jnp.float32


def kernel(
    tok_ref, gain_ref, inw_ref, short_ref, filt_ref, skip_ref, outw_ref,
    out_ref,
    xg, ag, wg, wo, mx, acc, acc2, gated, toep, ext, ss, hs_send, hs_recv,
    xs, xr, ms, mr, wsend, wrecv, wsib, osend, orecv, osib, hs, hr,
):
    ctx = lax.axis_index("ctx")
    mp = lax.axis_index("mp")
    core = ctx % 2
    z = (ctx // 2) % NZ
    yl = ctx // (2 * NZ)
    x = mp % NX
    yh = mp // NX

    def at(yl_, z_, core_, yh_, x_):
        return ((yl_ * NZ + z_) * 2 + core_, yh_ * NX + x_)

    right = at(yl, z, core, yh, (x + 1) % NX)
    left = at(yl, z, core, yh, (x + NX - 1) % NX)
    across = at(yl, z, core, 1 - yh, x)
    up = at(yl, (z + 1) % NZ, core, yh, x)
    down = at(yl, (z + NZ - 1) % NZ, core, yh, x)
    beside = at(1 - yl, z, core, yh, x)
    sib = at(yl, z, 1 - core, yh, x)
    after = ((ctx + 1) % (4 * NZ), mp)
    before = ((ctx + 4 * NZ - 1) % (4 * NZ), mp)

    barrier = pltpu.get_barrier_semaphore()
    everyone = (right, left, across, up, down, beside, sib, after, before)
    for dev in everyone:
        pl.semaphore_signal(barrier, inc=1, device_id=dev, device_id_type=pl.DeviceIdType.MESH)

    own = mp
    xg[own, 0:ROWS, :] = tok_ref[...]
    gain = gain_ref[...]
    g_hi = gain.astype(BF).astype(F32)
    g_mid = (gain - g_hi).astype(BF).astype(F32)
    g_lo = gain - g_hi - g_mid
    which = lax.broadcasted_iota(jnp.int32, (16, COLS), 0)
    parts = jnp.where(which == 0, g_hi, jnp.where(which == 1, g_mid, jnp.where(which == 2, g_lo, 0.0)))
    xg[own, ROWS:XROWS, :] = parts.astype(BF)

    pl.semaphore_wait(barrier, len(everyone))

    sends = []

    def push(src, dst, ssem, rsem, dev):
        copy = pltpu.make_async_remote_copy(
            src_ref=src, dst_ref=dst, send_sem=ssem, recv_sem=rsem,
            device_id=dev, device_id_type=pl.DeviceIdType.MESH,
        )
        copy.start()
        sends.append(copy)

    def arrived(dst, ssem, rsem):
        pltpu.make_async_remote_copy(
            src_ref=dst, dst_ref=dst, send_sem=ssem, recv_sem=rsem,
            device_id=sib, device_id_type=pl.DeviceIdType.MESH,
        ).wait_recv()

    class Ring:
        def __init__(self, buf, ssem, rsem, halves):
            self.buf, self.ssem, self.rsem = buf, ssem, rsem
            self.halves = halves
            self.count = 0

        def view(self, plane, dx, half):
            slot = ((yh + plane) % NY) * NX + (x + dx) % NX
            begin, size = self.halves[half]
            return self.buf.at[slot, pl.ds(begin, size), :]

        def send(self, plane, dx, half, way):
            dev, shift = {"r": (right, 1), "l": (left, NX - 1), "y": (across, 0)}[way]
            there = (1, 0) if way == "y" else (plane, (dx + NX - shift) % NX)
            view = self.view(plane, dx, half)
            push(
                view, view, self.ssem.at[self.count],
                self.rsem.at[there[0], there[1], half], dev,
            )
            self.count += 1

        def wait(self, plane, dx, half):
            arrived(self.view(plane, dx, half), self.ssem.at[0], self.rsem.at[plane, dx, half])

    class Column:
        def __init__(self, src, view_of, ssem, rsem, sibsem):
            self.src, self.view_of = src, view_of
            self.ssem, self.rsem, self.sibsem = ssem, rsem, sibsem
            self.count = 0

        def view(self, plane, dz, parity, part=None):
            q = ((yl + plane) % NY) * NZ + (z + dz) % NZ
            return self.view_of(2 * q + parity, part)

        def send(self, plane, dz, way, part=None):
            dev, shift = {"u": (up, 1), "d": (down, NZ - 1), "y": (beside, 0), "s": (sib, 0)}[way]
            dst = self.view(plane, dz, core, part)
            src = self.src if plane == 0 and dz == 0 else dst
            if way == "s":
                rsem = self.sibsem.at[plane, dz]
            elif way == "y":
                rsem = self.rsem.at[1, 0]
            else:
                rsem = self.rsem.at[plane, (dz + NZ - shift) % NZ + (NZ // 2 if part == 1 else 0)]
            push(src, dst, self.ssem.at[self.count], rsem, dev)
            self.count += 1

        def wait(self, plane, dz, part=None):
            arrived(
                self.view(plane, dz, core, part), self.ssem.at[0],
                self.rsem.at[plane, dz + (NZ // 2 if part == 1 else 0)],
            )

        def wait_sib(self, plane, dz):
            arrived(self.view(plane, dz, 1 - core), self.ssem.at[0], self.sibsem.at[plane, dz])

        def start(self):
            for way in ("y", "u", "d", "s"):
                self.send(0, 0, way)

        def beside_in(self):
            self.wait(1, 0)
            for way in ("u", "d", "s"):
                self.send(1, 0, way)

        def hop(self, plane, dist):
            for dz, way, part in ((NZ - dist, "u", 0), (dist, "d", 1)):
                self.wait(plane, dz)
                self.send(plane, dz, way, part if dist == NZ // 2 - 1 else None)
                self.send(plane, dz, "s")

        def last(self, plane):
            self.wait(plane, NZ // 2, 0)
            self.wait(plane, NZ // 2, 1)
            self.send(plane, NZ // 2, "s")

    def w_view(c, part):
        begin, size = (c % 4) * DEPTH, DEPTH
        if part is not None:
            begin, size = begin + part * (DEPTH // 2), DEPTH // 2
        return wg.at[c // 4, :, pl.ds(begin, size), :]

    def o_view(c, part):
        begin, size = (c % 4) * DEPTH, DEPTH
        if part is not None:
            begin, size = begin + part * (DEPTH // 2), DEPTH // 2
        return wo.at[c // 4, pl.ds(begin, size), :]

    tok = Ring(xg, xs, xr, ((0, HALF), (HALF, XROWS - HALF)))
    mix = Ring(mx, ms, mr, ((HALF, HALF), (0, HALF)))
    win = Column(inw_ref, w_view, wsend, wrecv, wsib)
    wout = Column(outw_ref, o_view, osend, orecv, osib)

    win.start()
    for half, way in ((0, "y"), (0, "r"), (1, "l"), (1, "y"), (1, "r"), (0, "l")):
        tok.send(0, 0, half, way)

    wg[ctx // 4, :, pl.ds(pl.multiple_of((ctx % 4) * DEPTH, DEPTH), DEPTH), :] = inw_ref[...]
    wo[ctx // 4, pl.ds(pl.multiple_of((ctx % 4) * DEPTH, DEPTH), DEPTH), :] = outw_ref[...]
    acc[...] = jnp.zeros_like(acc)
    ss[...] = jnp.zeros_like(ss)
    acc2[...] = tok_ref[...].astype(F32)
    ext[:, 0:BLK] = filt_ref[...].astype(F32)
    ext[:, BLK:] = jnp.zeros((ext.shape[0], BLK), F32)

    @pl.loop(0, ext.shape[0])
    def _(g):
        row = jnp.broadcast_to(ext[pl.ds(g, 1), :], (2 * BLK, 2 * BLK))
        shifted = pltpu.roll(row, BLK, 1, stride=1, stride_axis=0)
        toep[pl.ds(pl.multiple_of(g * BLK, BLK), BLK), :] = shifted[:, 0:BLK].T.astype(BF)

    def norm(plane, dx):
        slot = ((yh + plane) % NY) * NX + (x + dx) % NX
        rows3 = xg[slot, ROWS:XROWS, :].astype(F32)
        g = rows3[0:1] + rows3[1:2] + rows3[2:3]

        @pl.loop(0, NB)
        def _(b):
            rows = pl.ds(pl.multiple_of(b * BLK, BLK), BLK)
            t = xg[slot, rows, :].astype(F32)
            sq = t * t
            ss[rows, :] += (sq[:, 0:128] + sq[:, 128:256]) + (sq[:, 256:384] + sq[:, 384:512])
            ag[slot, rows, :] = (t * g).astype(BF)

    norm(0, 0)

    win.beside_in()
    win.hop(0, 1)
    tok.wait(0, NX - 1, 0)
    tok.send(0, NX - 1, 0, "r")
    tok.wait(0, 1, 1)
    tok.send(0, 1, 1, "l")
    tok.wait(1, 0, 0)
    tok.send(1, 0, 0, "r")
    tok.wait(1, 0, 1)
    tok.send(1, 0, 1, "l")
    tok.send(1, 0, 1, "r")
    tok.send(1, 0, 0, "l")
    win.hop(1, 1)
    norm(1, 0)
    tok.wait(0, NX - 1, 1)
    norm(0, NX - 1)
    tok.wait(0, 1, 0)
    norm(0, 1)
    win.hop(0, 2)
    tok.wait(0, 2, 0)
    tok.wait(0, 2, 1)
    norm(0, 2)
    win.hop(1, 2)
    tok.wait(1, NX - 1, 0)
    tok.send(1, NX - 1, 0, "r")
    tok.wait(1, 1, 1)
    tok.send(1, 1, 1, "l")
    win.hop(0, 3)
    tok.wait(1, NX - 1, 1)
    norm(1, NX - 1)
    tok.wait(1, 1, 0)
    norm(1, 1)
    win.hop(1, 3)
    wout.start()
    tok.wait(1, 2, 0)
    tok.wait(1, 2, 1)
    norm(1, 2)
    for plane in range(NY):
        for dz in range(NZ):
            if dz != NZ // 2:
                win.wait_sib(plane, dz)

    def project(begin, count):
        @pl.loop(0, count * 3)
        def _(i):
            k = begin + i // 3
            s = i % 3
            plane, off = k % 2, k // 2
            off = jnp.where(off == 2, 3, jnp.where(off == 3, 2, off))
            m = ((yl + plane) % NY) * 4 + (z // 2 + off) % 4
            acc[s, 8 : 8 + ROWS, :] += jnp.dot(ag[m], wg[m, s], preferred_element_type=F32)

    project(0, 6)
    win.last(0)
    win.last(1)
    win.wait_sib(0, NZ // 2)
    win.wait_sib(1, NZ // 2)
    project(6, 2)

    wout.beside_in()
    wout.hop(0, 1)

    lanes_group = lax.broadcasted_iota(jnp.int32, (BLK, 128), 1) // GSIZE

    def taps(s, b, j):
        cols = slice(128 * j, 128 * (j + 1))
        v = acc[s, pl.ds(pl.multiple_of(b * BLK, BLK), BLK + 8), cols]
        total = short_ref[0, s : s + 1, cols] * v
        total = total + short_ref[1, s : s + 1, cols] * pltpu.roll(v, 1, 0)
        total = total + short_ref[2, s : s + 1, cols] * pltpu.roll(v, 2, 0)
        return total[8:]

    def settle(b):
        rows = pl.ds(pl.multiple_of(b * BLK, BLK), BLK)
        scale = lax.rsqrt(jnp.sum(ss[rows, :], axis=1, keepdims=True) / D + EPS)
        at_ = pl.ds(pl.multiple_of(b * BLK + 8, 8), BLK)
        for s in range(3):
            acc[s, at_, :] = (acc[s, at_, :] * scale).astype(BF).astype(F32)

    def gate(b):
        for j in range(4):
            kv = taps(1, b, j) * taps(2, b, j)
            gated[pl.ds(pl.multiple_of((b + 1) * BLK, BLK), BLK), 128 * j : 128 * (j + 1)] = kv.astype(BF)

    def combine(b):
        rows = pl.ds(pl.multiple_of(b * BLK, BLK), BLK)
        for j in range(4):
            cols = slice(128 * j, 128 * (j + 1))
            window = gated[pl.ds(pl.multiple_of(b * BLK, BLK), 2 * BLK), cols]
            every = jnp.dot(toep[1024 * j : 1024 * (j + 1), :], window, preferred_element_type=F32)
            medium = every[0:BLK]
            for g in range(1, 8):
                medium = jnp.where(lanes_group == g, every[BLK * g : BLK * (g + 1)], medium)
            direct = window[BLK:].astype(F32)
            mixed = taps(0, b, j) * (medium + skip_ref[:, cols] * direct)
            mx[own, rows, cols] = mixed.astype(BF)

    halo_g = (gated.at[pl.ds(ROWS, BLK), :], gated.at[pl.ds(0, BLK), :])

    def halo_out():
        for s in range(3):
            hs_send[s] = acc[s, ROWS - 8 : ROWS + 8, :].astype(BF)
        push(hs_send, hs_recv, hs.at[0], hr.at[0], after)
        push(halo_g[0], halo_g[1], hs.at[1], hr.at[1], after)

    def halo_in():
        arrived(hs_recv, hs.at[0], hr.at[0])
        arrived(halo_g[1], hs.at[1], hr.at[1])
        inside = ctx > 0
        for s in range(3):
            acc[s, 0:8, :] = jnp.where(inside, hs_recv[s].astype(F32)[8:16], 0.0)
        gated[0:BLK, :] = jnp.where(inside, gated[0:BLK, :].astype(F32), 0.0).astype(BF)

    settle(5)
    settle(4)
    gate(5)
    halo_out()
    settle(3)
    gate(4)
    combine(5)
    settle(2)
    gate(3)
    combine(4)
    settle(1)
    gate(2)
    combine(3)
    for way in ("y", "r", "l"):
        mix.send(0, 0, 0, way)
    settle(0)
    gate(1)
    combine(2)
    halo_in()
    gate(0)
    combine(1)
    combine(0)
    for way in ("y", "r", "l"):
        mix.send(0, 0, 1, way)

    def outward(plane, dx):
        slot = ((yh + plane) % NY) * NX + (x + dx) % NX
        acc2[...] += jnp.dot(mx[slot], wo[slot], preferred_element_type=F32)

    wout.hop(1, 1)
    mix.wait(0, NX - 1, 0)
    mix.send(0, NX - 1, 0, "r")
    mix.wait(1, 0, 0)
    mix.send(1, 0, 0, "r")
    mix.send(1, 0, 0, "l")
    wout.hop(0, 2)
    wout.hop(1, 2)
    mix.wait(0, 1, 1)
    mix.send(0, 1, 1, "l")
    mix.wait(1, 0, 1)
    mix.send(1, 0, 1, "r")
    mix.send(1, 0, 1, "l")
    wout.hop(0, 3)
    wout.hop(1, 3)
    wout.last(0)
    wout.last(1)
    for plane in range(NY):
        for dz in range(NZ):
            wout.wait_sib(plane, dz)
    mix.wait(0, NX - 1, 1)
    mix.wait(0, 1, 0)
    mix.wait(1, NX - 1, 0)
    mix.send(1, NX - 1, 0, "r")
    mix.wait(1, 1, 1)
    mix.send(1, 1, 1, "l")
    outward(0, 0)
    outward(1, 0)
    outward(0, NX - 1)
    outward(0, 1)
    mix.wait(0, 2, 0)
    mix.wait(0, 2, 1)
    outward(0, 2)
    mix.wait(1, NX - 1, 1)
    outward(1, NX - 1)
    mix.wait(1, 1, 0)
    outward(1, 1)
    mix.wait(1, 2, 0)
    mix.wait(1, 2, 1)
    outward(1, 2)
    out_ref[...] = acc2[...].astype(BF)
    for copy in sends:
        copy.wait_send()


def body(tokens, norm_gain, in_weight, short_weight, filters, skip, out_weight):
    vmem = pl.BlockSpec(memory_space=pltpu.VMEM)
    dma = pltpu.SemaphoreType.DMA
    return pl.pallas_call(
        kernel,
        out_shape=jax.ShapeDtypeStruct((ROWS, COLS), BF),
        in_specs=[vmem] * 7,
        out_specs=vmem,
        scratch_shapes=[
            pltpu.VMEM((8, XROWS, COLS), BF),
            pltpu.VMEM((8, ROWS, COLS), BF),
            pltpu.VMEM((8, 3, COLS, COLS), BF),
            pltpu.VMEM((8, COLS, COLS), BF),
            pltpu.VMEM((8, ROWS, COLS), BF),
            pltpu.VMEM((3, ROWS + 8, COLS), F32),
            pltpu.VMEM((ROWS, COLS), F32),
            pltpu.VMEM((ROWS + BLK, COLS), BF),
            pltpu.VMEM((32 * BLK, 2 * BLK), BF),
            pltpu.VMEM((32, 2 * BLK), F32),
            pltpu.VMEM((ROWS, 128), F32),
            pltpu.VMEM((3, 16, COLS), BF),
            pltpu.VMEM((3, 16, COLS), BF),
            dma((14,)), dma((2, 4, 2)),
            dma((14,)), dma((2, 4, 2)),
            dma((40,)), dma((2, 9)), dma((2, 8)),
            dma((40,)), dma((2, 9)), dma((2, 8)),
            dma((2,)), dma((2,)),
        ],
        compiler_params=pltpu.CompilerParams(
            collective_id=0, has_side_effects=True, vmem_limit_bytes=60 * 1024 * 1024
        ),
    )(
        tokens,
        norm_gain.reshape(1, COLS),
        jnp.transpose(in_weight, (1, 0, 2)),
        short_weight,
        filters.T,
        skip.reshape(1, COLS),
        out_weight,
    )


def solution(mesh):
    return jax.shard_map(
        body,
        mesh=mesh,
        in_specs=(
            P("ctx", "mp"),
            P("mp"),
            P("ctx", None, "mp"),
            P(None, None, "mp"),
            P(None, "mp"),
            P("mp"),
            P("ctx", "mp"),
        ),
        out_specs=P("ctx", "mp"),
        check_vma=False,
    )
```

time: 389 us -> 143 us (0.37)
  waiting for transfers between devices: 289 us -> 0 us
  Pallas kernels: 0 us -> 141 us
  matrix products: 34.9 us -> 0 us
  blocking collectives: 28.4 us -> 0 us
  between operations: 13.3 us -> 0.01 us
  other arithmetic: 9.79 us -> 0 us
  local copies, waits for them, and re-layouts: 9.2 us -> 2.06 us
    all_gather x4 -> x0, waiting for transfers between devices: 287 us -> none  [the longest x1 105 us: body(): mixed_rows = lax.all_gather(mixed, 'mp', axis=1, tiled=True)]
    pallas_call x0 -> x1, Pallas kernels: none -> 141 us  [body(): pl.pallas_call(kernel, out_shape=jax.ShapeDtypeStruct((ROWS, COLS), BF),...]
    dot_general x4 -> x0, matrix products: 34.9 us -> none  [the longest x1 14.9 us: body(): jnp.einsum('tk,qkc->tqc', normed, lax.all_gather(jnp.transpose(in_weight,...]
    all_gather x1 -> x0, blocking collectives: 28.4 us -> none  [body(): gain = lax.all_gather(norm_gain, 'mp', axis=0, tiled=True)]
    reduce_sum x1 -> x0, other arithmetic: 4.07 us -> none  [body(): squares = jnp.sum(rows_f * rows_f, axis=1)]
  transfers between devices with their start and end apart: 5 -> 0, of which waited for: 4 -> 0; matrix products, arithmetic and copies ran while one was open for 11% -> 0% of each run, Pallas kernels for 0% -> 0%
where the time goes in v2:
time: 143 us
  Pallas kernels  141 us (99%)
  local copies, waits for them, and re-layouts  2.06 us (1%)
    pallas_call x1, Pallas kernels, body(): pl.pallas_call(kernel, out_shape=jax.ShapeDtypeStruct((ROWS, COLS), BF),...  141 us

profile of v2, /device:TPU:4, one launch (start us, length us, event | category | flops | bytes accessed | tf_op | source)
XLA Modules:
  0.0 142.9 jit_solution(18288149428675031889)
XLA Ops:
  0.0 140.8 %shard_map.73 = bf16[768,512]{1,0:T(8,128)(2,1)} custom-call(bf16[768,512]{1,0:T(8,128)(2,1)} %tok_ref.1, f32[1,512]{1,0:T(1,128)} %bitcast.6, bf16[3,128,512]{2,1,0:T(8,128)(2,1)} %bitcast.4, f32[3,3,512]{2,1,0:T(4,128)} %short_ref.1, bf16[32,128]{1,0:T(8,128)(2,1)} %bitcast.5, f32[1,512]{1,0:T(1,128)} %bitcast.7, bf16[128,512]{1,0:T(8,128)(2,1)} %outw_ref.1), custom_call_target="tpu_custom_call" | custom-call | tf_op jit(solution)/shard_map/pallas_call | solution.py:397
  140.9 2.1 %copy.9 = bf16[768,512]{1,0:T(8,128)(2,1)} copy(bf16[768,512]{1,0:T(8,128)(2,1)} %shard_map.73) | data formatting | bytes 1572864

commit v3 on v2

v3 whole, which is shorter than its diff:
```python
import jax
import jax.numpy as jnp
from jax import lax
from jax.experimental import pallas as pl
from jax.experimental.pallas import tpu as pltpu
from jax.sharding import PartitionSpec as P

D = 4096
EPS = 1e-06
NX, NZ, NY = 4, 8, 2
ROWS, COLS, DEPTH = 768, 512, 128
BLK = 128
NB = ROWS // BLK
XROWS = ROWS + 16
HALF = 384
GSIZE = 16
NEAR = 2
CHUNK = 2 * BLK
BF = jnp.bfloat16
F32 = jnp.float32


def kernel(
    tok_ref, gain_ref, inw_ref, short_ref, filt_ref, skip_ref, outw_ref,
    out_ref,
    xg, ag, wg, wo, yo, mx, acc, acc2, gated, toep, ext, ss, hs_send, hs_recv,
    part_send, part_recv, out_v, gain_v, short_v, filt_v, skip_v,
    ls, xs, xr, ms, mr, wsend, wrecv, wsib, osend, orecv, osib, ys, yr, ps, pr, hs, hr,
):
    ctx = lax.axis_index("ctx")
    mp = lax.axis_index("mp")
    core = ctx % 2
    z = (ctx // 2) % NZ
    yl = ctx // (2 * NZ)
    x = mp % NX
    yh = mp // NX

    def at(yl_, z_, core_, yh_, x_):
        return ((yl_ * NZ + z_) * 2 + core_, yh_ * NX + x_)

    right = at(yl, z, core, yh, (x + 1) % NX)
    left = at(yl, z, core, yh, (x + NX - 1) % NX)
    across = at(yl, z, core, 1 - yh, x)
    up = at(yl, (z + 1) % NZ, core, yh, x)
    down = at(yl, (z + NZ - 1) % NZ, core, yh, x)
    beside = at(1 - yl, z, core, yh, x)
    corner = at(1 - yl, z, core, 1 - yh, x)
    sib = at(yl, z, 1 - core, yh, x)
    after = ((ctx + 1) % (4 * NZ), mp)
    before = ((ctx + 4 * NZ - 1) % (4 * NZ), mp)

    barrier = pltpu.get_barrier_semaphore()
    everyone = (right, left, across, up, down, beside, corner, sib, after, before)
    for dev in everyone:
        pl.semaphore_signal(barrier, inc=1, device_id=dev, device_id_type=pl.DeviceIdType.MESH)

    own = mp
    row = yl * NZ + z
    my_rows = pl.ds(pl.multiple_of(core * DEPTH, DEPTH), DEPTH)
    loads = [
        pltpu.make_async_copy(src, dst, ls.at[i])
        for i, (src, dst) in enumerate((
            (inw_ref, wg.at[row, :, my_rows, :]),
            (tok_ref, xg.at[own, pl.ds(0, ROWS), :]),
            (gain_ref, gain_v),
            (outw_ref, yo.at[2 * yh + yl]),
            (filt_ref, filt_v),
            (short_ref, short_v),
            (skip_ref, skip_v),
        ))
    ]
    for copy in loads:
        copy.start()

    loads[2].wait()
    gain = gain_v[...]
    g_hi = gain.astype(BF).astype(F32)
    g_mid = (gain - g_hi).astype(BF).astype(F32)
    g_lo = gain - g_hi - g_mid
    which = lax.broadcasted_iota(jnp.int32, (16, COLS), 0)
    parts = jnp.where(which == 0, g_hi, jnp.where(which == 1, g_mid, jnp.where(which == 2, g_lo, 0.0)))
    xg[own, ROWS:XROWS, :] = parts.astype(BF)
    loads[0].wait()
    loads[1].wait()

    pl.semaphore_wait(barrier, len(everyone))

    sends = []

    def push(src, dst, ssem, rsem, dev):
        copy = pltpu.make_async_remote_copy(
            src_ref=src, dst_ref=dst, send_sem=ssem, recv_sem=rsem,
            device_id=dev, device_id_type=pl.DeviceIdType.MESH,
        )
        copy.start()
        sends.append(copy)

    def arrived(dst, ssem, rsem):
        pltpu.make_async_remote_copy(
            src_ref=dst, dst_ref=dst, send_sem=ssem, recv_sem=rsem,
            device_id=sib, device_id_type=pl.DeviceIdType.MESH,
        ).wait_recv()

    class Ring:
        def __init__(self, buf, planes, ssem, rsem, pieces):
            self.buf, self.planes = buf, planes
            self.ssem, self.rsem, self.pieces = ssem, rsem, pieces
            self.count = 0

        def slot(self, plane, dx):
            return ((yh + plane) % NY if self.planes == 2 else 0) * NX + (x + dx) % NX

        def view(self, plane, dx, piece):
            begin, size = self.pieces[piece]
            return self.buf.at[self.slot(plane, dx), pl.ds(begin, size), :]

        def send(self, plane, dx, piece, way):
            dev, shift = {"r": (right, 1), "l": (left, NX - 1), "y": (across, 0)}[way]
            there = (1, 0) if way == "y" else (plane, (dx + NX - shift) % NX)
            view = self.view(plane, dx, piece)
            push(
                view, view, self.ssem.at[self.count],
                self.rsem.at[there[0], there[1], piece], dev,
            )
            self.count += 1

        def wait(self, plane, dx, piece):
            arrived(self.view(plane, dx, piece), self.ssem.at[0], self.rsem.at[plane, dx, piece])

    class Column:
        def __init__(self, view_of, ssem, rsem, sibsem, near):
            self.view_of = view_of
            self.ssem, self.rsem, self.sibsem, self.near = ssem, rsem, sibsem, near
            self.count = 0

        def view(self, plane, dz, parity, part=None):
            begin, size = parity * DEPTH, DEPTH
            if part is not None:
                begin, size = begin + part * (DEPTH // 2), DEPTH // 2
            return self.view_of(plane, (z + dz) % NZ, pl.ds(begin, size))

        def send(self, plane, dz, way, part=None):
            dev, shift = {"u": (up, 1), "d": (down, NZ - 1), "y": (beside, 0), "s": (sib, 0)}[way]
            view = self.view(plane, dz, core, part)
            if way == "s":
                rsem = self.sibsem.at[plane, dz]
            elif way == "y":
                rsem = self.rsem.at[1, dz, 0]
            else:
                rsem = self.rsem.at[plane, (dz + NZ - shift) % NZ, part]
            push(view, view, self.ssem.at[self.count], rsem, dev)
            self.count += 1

        def wait(self, plane, dz, part=None):
            arrived(
                self.view(plane, dz, core, part), self.ssem.at[0],
                self.rsem.at[plane, dz, 0 if part is None else part],
            )

        def wait_sib(self, plane, dz):
            arrived(self.view(plane, dz, 1 - core), self.ssem.at[0], self.sibsem.at[plane, dz])

        def start(self, plane):
            for part in (0, 1):
                self.send(plane, 0, "u", part)
                self.send(plane, 0, "d", 1 - part)

        def hop(self, plane, dist):
            near = NZ // 2 if plane == 0 else self.near
            for turn in (0, 1):
                for dz, way, part in ((NZ - dist, "u", turn), (dist, "d", 1 - turn)):
                    self.wait(plane, dz, part)
                    if dist < near and (dist < NZ // 2 - 1 or turn == 0):
                        self.send(plane, dz, way, part)
            for dz in (NZ - dist, dist):
                self.out(plane, dz, dist)

        def out(self, plane, dz, dist):
            if plane == 0 and dist > self.near:
                self.send(0, dz, "y")
            self.send(plane, dz, "s")

        def last(self, plane):
            self.wait(plane, NZ // 2, 0)
            self.wait(plane, NZ // 2, 1)
            self.out(plane, NZ // 2, NZ // 2)

    tok = Ring(xg, 2, xs, xr, ((0, HALF), (HALF, XROWS - HALF)))
    mix = Ring(mx, 1, ms, mr, tuple((BLK * b, BLK) for b in range(NB)))
    win = Column(
        lambda plane, z_, rows: wg.at[((yl + plane) % NY) * NZ + z_, :, rows, :],
        wsend, wrecv, wsib, NEAR,
    )
    wout = Column(
        lambda plane, z_, rows: wo.at[plane, z_, rows, :],
        osend, orecv, osib, NZ // 2,
    )

    win.send(0, 0, "y")
    win.start(0)
    for half, way in ((0, "y"), (0, "r"), (1, "l"), (1, "y"), (1, "r"), (0, "l")):
        tok.send(0, 0, half, way)
    win.send(0, 0, "s")
    for copy in loads[3:]:
        copy.wait()
    mine = yo.at[2 * yh + yl]
    for i, dev in enumerate((beside, across, corner)):
        push(mine, mine, ys.at[i], yr.at[i], dev)

    acc[...] = jnp.zeros_like(acc)
    ss[...] = jnp.zeros_like(ss)

    def norm(plane, dx):
        slot = tok.slot(plane, dx)
        rows3 = xg[slot, ROWS:XROWS, :].astype(F32)
        g = rows3[0:1] + rows3[1:2] + rows3[2:3]

        @pl.loop(0, NB)
        def _(b):
            rows = pl.ds(pl.multiple_of(b * BLK, BLK), BLK)
            t = xg[slot, rows, :].astype(F32)
            sq = t * t
            ss[rows, :] += (sq[:, 0:128] + sq[:, 128:256]) + (sq[:, 256:384] + sq[:, 384:512])
            a = (t * g).astype(BF)
            ag[2 * slot, rows, :] = a[:, 0:256]
            ag[2 * slot + 1, rows, :] = a[:, 256:512]

    def spread_filters():
        ext[:, 0:BLK] = filt_v[...].astype(F32)
        ext[:, BLK:] = jnp.zeros((ext.shape[0], BLK), F32)

        @pl.loop(0, ext.shape[0])
        def _(g):
            row_ = jnp.broadcast_to(ext[pl.ds(g, 1), :], (2 * BLK, 2 * BLK))
            shifted = pltpu.roll(row_, BLK, 1, stride=1, stride_axis=0)
            toep[pl.ds(pl.multiple_of(g * BLK, BLK), BLK), :] = shifted[:, 0:BLK].T.astype(BF)

    opposite = tok.slot(0, 2)
    opposite_there = tok.slot(1, 2)

    def project(count, q_of, when):
        @pl.loop(0, count)
        def _(k):
            q = q_of(k)

            @pl.when(when(q))
            def _():
                @pl.loop(0, 3)
                def _(s):
                    acc[s, 8 : 8 + ROWS, :] += jnp.dot(ag[q], wg[q, s], preferred_element_type=F32)

    norm(0, 0)
    win.hop(0, 1)
    win.wait(1, 0)
    win.send(1, 0, "s")
    spread_filters()
    win.hop(0, 2)
    tok.wait(1, 0, 0)
    tok.send(1, 0, 0, "r")
    tok.wait(1, 0, 1)
    tok.send(1, 0, 1, "l")
    tok.send(1, 0, 1, "r")
    tok.send(1, 0, 0, "l")
    win.hop(0, 3)
    win.start(1)
    for dx in (NX - 1, 1):
        tok.wait(0, dx, 0)
        tok.wait(0, dx, 1)
        norm(0, dx)
    norm(1, 0)
    win.last(0)
    tok.wait(1, NX - 1, 0)
    tok.send(1, NX - 1, 0, "r")
    tok.wait(1, 1, 1)
    tok.send(1, 1, 1, "l")
    for i, (l_, h_) in enumerate(((1 - yl, yh), (yl, 1 - yh), (1 - yl, 1 - yh))):
        arrived(yo.at[2 * h_ + l_], ys.at[i], yr.at[i])
    for plane in range(NY):
        wo[plane, z, my_rows, :] = yo[2 * plane + yh]
    win.hop(1, 1)
    tok.send(0, NX - 1, 0, "r")
    tok.send(0, 1, 1, "l")
    for plane in range(NY):
        wout.start(plane)
        wout.send(plane, 0, "s")
    tok.wait(1, NX - 1, 1)
    norm(1, NX - 1)
    tok.wait(1, 1, 0)
    norm(1, 1)
    for dz in range(NZ):
        win.wait_sib(0, dz)
    project(
        8, lambda k: yl * NZ + k,
        lambda q: jnp.logical_and(q // 2 != opposite, q // 2 != opposite_there),
    )
    for dz in (5, 3):
        win.wait(1, dz)
        win.send(1, dz, "s")
    win.hop(1, 2)
    for plane in range(NY):
        wout.hop(plane, 1)
    tok.wait(1, 2, 0)
    tok.wait(1, 2, 1)
    norm(1, 2)
    project(2, lambda k: 2 * opposite_there + k, lambda q: yh != yl)
    for dz in (0, 1, 7, 2, 6, 5, 3):
        win.wait_sib(1, dz)
    project(
        7, lambda k: (1 - yl) * NZ + (z + k + (k > 3).astype(jnp.int32)) % NZ,
        lambda q: q // 2 != opposite,
    )
    win.wait(1, 4)
    win.send(1, 4, "s")
    tok.wait(0, 2, 0)
    tok.wait(0, 2, 1)
    norm(0, 2)
    project(2, lambda k: 2 * opposite + k, lambda q: q != (1 - yl) * NZ + (z + 4) % NZ)
    for plane in range(NY):
        wout.hop(plane, 2)
    win.wait_sib(1, 4)
    project(1, lambda k: (1 - yl) * NZ + (z + 4) % NZ, lambda q: q >= 0)

    lanes_group = lax.broadcasted_iota(jnp.int32, (BLK, 128), 1) // GSIZE

    def taps(s, b, j):
        cols = slice(128 * j, 128 * (j + 1))
        v = acc[s, pl.ds(pl.multiple_of(b * BLK, BLK), BLK + 8), cols]
        total = short_v[0, s : s + 1, cols] * v
        total = total + short_v[1, s : s + 1, cols] * pltpu.roll(v, 1, 0)
        total = total + short_v[2, s : s + 1, cols] * pltpu.roll(v, 2, 0)
        return total[8:]

    def settle(b):
        rows = pl.ds(pl.multiple_of(b * BLK, BLK), BLK)
        scale = lax.rsqrt(jnp.sum(ss[rows, :], axis=1, keepdims=True) / D + EPS)
        at_ = pl.ds(pl.multiple_of(b * BLK + 8, 8), BLK)
        for s in range(3):
            acc[s, at_, :] = (acc[s, at_, :] * scale).astype(BF).astype(F32)

    def gate(b):
        for j in range(4):
            kv = taps(1, b, j) * taps(2, b, j)
            gated[pl.ds(pl.multiple_of((b + 1) * BLK, BLK), BLK), 128 * j : 128 * (j + 1)] = kv.astype(BF)

    def combine(b):
        rows = pl.ds(pl.multiple_of(b * BLK, BLK), BLK)
        for j in range(4):
            cols = slice(128 * j, 128 * (j + 1))
            window = gated[pl.ds(pl.multiple_of(b * BLK, BLK), 2 * BLK), cols]
            every = jnp.dot(toep[1024 * j : 1024 * (j + 1), :], window, preferred_element_type=F32)
            medium = every[0:BLK]
            for g in range(1, 8):
                medium = jnp.where(lanes_group == g, every[BLK * g : BLK * (g + 1)], medium)
            direct = window[BLK:].astype(F32)
            mixed = taps(0, b, j) * (medium + skip_v[:, cols] * direct)
            mx[x, rows, cols] = mixed.astype(BF)

    halo_g = (gated.at[pl.ds(ROWS, BLK), :], gated.at[pl.ds(0, BLK), :])

    def halo_out():
        for s in range(3):
            hs_send[s] = acc[s, ROWS - 8 : ROWS + 8, :].astype(BF)
        push(hs_send, hs_recv, hs.at[0], hr.at[0], after)
        push(halo_g[0], halo_g[1], hs.at[1], hr.at[1], after)

    def halo_in():
        arrived(hs_recv, hs.at[0], hr.at[0])
        arrived(halo_g[1], hs.at[1], hr.at[1])
        inside = ctx > 0
        for s in range(3):
            acc[s, 0:8, :] = jnp.where(inside, hs_recv[s].astype(F32)[8:16], 0.0)
        gated[0:BLK, :] = jnp.where(inside, gated[0:BLK, :].astype(F32), 0.0).astype(BF)

    def give(b):
        for way in ("r", "l") if b % 2 else ("l", "r"):
            mix.send(0, 0, b, way)

    def relay(b):
        mix.wait(0, NX - 1, b)
        mix.send(0, NX - 1, b, "r")
        mix.wait(0, 1, b - 1)
        mix.send(0, 1, b - 1, "l")

    settle(5)
    settle(4)
    gate(5)
    halo_out()
    settle(3)
    gate(4)
    combine(5)
    give(5)
    settle(2)
    gate(3)
    combine(4)
    give(4)
    settle(1)
    gate(2)
    combine(3)
    settle(0)
    gate(1)
    combine(2)
    halo_in()
    gate(0)
    combine(1)
    combine(0)
    relay(5)
    give(3)
    give(2)
    for plane in range(NY):
        wout.hop(plane, 3)

    def product(plane, c):
        total = None
        for x_ in range(NX):
            w = wo[plane, 2 * x_ : 2 * x_ + 2].reshape(COLS, COLS)
            term = jnp.dot(mx[x_, CHUNK * c : CHUNK * (c + 1), :], w, preferred_element_type=F32)
            total = term if total is None else total + term
        return total

    def outward(c):
        b = 2 * c + 1
        for dx, piece in ((NX - 1, b - 1), (1, b), (2, b), (2, b - 1)):
            mix.wait(0, dx, piece)
        rows = slice(CHUNK * c, CHUNK * (c + 1))
        part_send[rows, :] = product(1 - yh, c).astype(BF)
        there = pl.ds(CHUNK * c, CHUNK)
        push(part_send.at[there, :], part_recv.at[there, :], ps.at[c], pr.at[c], across)
        acc2[rows, :] = xg[own, rows, :].astype(F32) + product(yh, c)

    def finish(c):
        there = pl.ds(CHUNK * c, CHUNK)
        rows = slice(CHUNK * c, CHUNK * (c + 1))
        arrived(part_recv.at[there, :], ps.at[c], pr.at[c])
        out_v[rows, :] = (acc2[rows, :] + part_recv[rows, :].astype(F32)).astype(BF)
        copy = pltpu.make_async_copy(out_v.at[there, :], out_ref.at[there, :], ls.at[c])
        copy.start()
        return copy

    relay(3)
    give(1)
    give(0)
    for plane in range(NY):
        wout.last(plane)
    for plane in range(NY):
        for dz in range(1, NZ):
            wout.wait_sib(plane, dz)
        wout.wait_sib(plane, 0)
    outward(2)
    relay(1)
    outward(1)
    outward(0)
    stores = [finish(2), finish(1), finish(0)]
    for copy in stores:
        copy.wait()
    for copy in sends:
        copy.wait_send()


def body(tokens, norm_gain, in_weight, short_weight, filters, skip, out_weight):
    dma = pltpu.SemaphoreType.DMA
    hbm = pl.BlockSpec(memory_space=pl.ANY)
    return pl.pallas_call(
        kernel,
        out_shape=jax.ShapeDtypeStruct((ROWS, COLS), BF),
        in_specs=[hbm] * 7,
        out_specs=hbm,
        scratch_shapes=[
            pltpu.VMEM((8, XROWS, COLS), BF),
            pltpu.VMEM((16, ROWS, 2 * DEPTH), BF),
            pltpu.VMEM((16, 3, 2 * DEPTH, COLS), BF),
            pltpu.VMEM((2, NZ, 2 * DEPTH, COLS), BF),
            pltpu.VMEM((4, DEPTH, COLS), BF),
            pltpu.VMEM((4, ROWS, COLS), BF),
            pltpu.VMEM((3, ROWS + 8, COLS), F32),
            pltpu.VMEM((ROWS, COLS), F32),
            pltpu.VMEM((ROWS + BLK, COLS), BF),
            pltpu.VMEM((32 * BLK, 2 * BLK), BF),
            pltpu.VMEM((32, 2 * BLK), F32),
            pltpu.VMEM((ROWS, 128), F32),
            pltpu.VMEM((3, 16, COLS), BF),
            pltpu.VMEM((3, 16, COLS), BF),
            pltpu.VMEM((ROWS, COLS), BF),
            pltpu.VMEM((ROWS, COLS), BF),
            pltpu.VMEM((ROWS, COLS), BF),
            pltpu.VMEM((1, COLS), F32),
            pltpu.VMEM((3, 3, COLS), F32),
            pltpu.VMEM((32, BLK), BF),
            pltpu.VMEM((1, COLS), F32),
            dma((7,)),
            dma((14,)), dma((2, 4, 2)),
            dma((18,)), dma((1, 4, 6)),
            dma((50,)), dma((2, 8, 2)), dma((2, 8)),
            dma((60,)), dma((2, 8, 2)), dma((2, 8)),
            dma((3,)), dma((3,)),
            dma((3,)), dma((3,)),
            dma((2,)), dma((2,)),
        ],
        compiler_params=pltpu.CompilerParams(
            collective_id=0, has_side_effects=True, vmem_limit_bytes=58 * 1024 * 1024
        ),
    )(
        tokens,
        norm_gain.reshape(1, COLS),
        jnp.transpose(in_weight, (1, 0, 2)),
        short_weight,
        filters.T,
        skip.reshape(1, COLS),
        out_weight,
    )


def solution(mesh):
    return jax.shard_map(
        body,
        mesh=mesh,
        in_specs=(
            P("ctx", "mp"),
            P("mp"),
            P("ctx", None, "mp"),
            P(None, None, "mp"),
            P(None, "mp"),
            P("mp"),
            P("ctx", "mp"),
        ),
        out_specs=P("ctx", "mp"),
        check_vma=False,
    )
```

time: 143 us -> 127 us (0.89)
  Pallas kernels: 141 us -> 125 us
    pallas_call x1, Pallas kernels: 141 us -> 125 us  [body(): pl.pallas_call(kernel, out_shape=jax.ShapeDtypeStruct((ROWS, COLS), BF),...]
where the time goes in v3:
time: 127 us
  Pallas kernels  125 us (98%)
  local copies, waits for them, and re-layouts  2.06 us (2%)
    pallas_call x1, Pallas kernels, body(): pl.pallas_call(kernel, out_shape=jax.ShapeDtypeStruct((ROWS, COLS), BF),...  125 us

profile of v3, /device:TPU:4, one launch (start us, length us, event | category | flops | bytes accessed | tf_op | source)
XLA Modules:
  0.0 126.8 jit_solution(8924085382394793717)
XLA Ops:
  0.0 124.7 %shard_map.73 = bf16[768,512]{1,0:T(8,128)(2,1)} custom-call(bf16[768,512]{1,0:T(8,128)(2,1)} %tok_ref.1, f32[1,512]{1,0:T(1,128)} %bitcast.6, bf16[3,128,512]{2,1,0:T(8,128)(2,1)} %bitcast.4, f32[3,3,512]{2,1,0:T(4,128)} %short_ref.1, bf16[32,128]{1,0:T(8,128)(2,1)} %bitcast.5, f32[1,512]{1,0:T(1,128)} %bitcast.7, bf16[128,512]{1,0:T(8,128)(2,1)} %outw_ref.1), custom_call_target="tpu_custom_call" | custom-call | tf_op jit(solution)/shard_map/pallas_call | solution.py:462
  124.7 2.1 %copy.9 = bf16[768,512]{1,0:T(8,128)(2,1)} copy(bf16[768,512]{1,0:T(8,128)(2,1)} %shard_map.73) | data formatting | bytes 1572864

commit v4 on v3

--- a/solution.py
+++ b/solution.py
@@ -14,8 +14,9 @@
 XROWS = ROWS + 16
 HALF = 384
 GSIZE = 16
-NEAR = 2
-CHUNK = 2 * BLK
+FAR = NZ // 2
+PIECES = ((640, 128), (512, 128), (384, 128), (256, 128), (192, 64), (128, 64), (64, 64), (0, 64))
+CHUNKS = ((512, 256), (256, 256), (128, 128), (0, 128))
 BF = jnp.bfloat16
 F32 = jnp.float32
 
@@ -63,7 +64,7 @@
             (inw_ref, wg.at[row, :, my_rows, :]),
             (tok_ref, xg.at[own, pl.ds(0, ROWS), :]),
             (gain_ref, gain_v),
-            (outw_ref, yo.at[2 * yh + yl]),
+            (outw_ref, yo.at[0]),
             (filt_ref, filt_v),
             (short_ref, short_v),
             (skip_ref, skip_v),
@@ -128,9 +129,9 @@
             arrived(self.view(plane, dx, piece), self.ssem.at[0], self.rsem.at[plane, dx, piece])
 
     class Column:
-        def __init__(self, view_of, ssem, rsem, sibsem, near):
+        def __init__(self, view_of, ssem, rsem, sibsem):
             self.view_of = view_of
-            self.ssem, self.rsem, self.sibsem, self.near = ssem, rsem, sibsem, near
+            self.ssem, self.rsem, self.sibsem = ssem, rsem, sibsem
             self.count = 0
 
         def view(self, plane, dz, parity, part=None):
@@ -145,7 +146,7 @@
             if way == "s":
                 rsem = self.sibsem.at[plane, dz]
             elif way == "y":
-                rsem = self.rsem.at[1, dz, 0]
+                rsem = self.rsem.at[1, dz, part or 0]
             else:
                 rsem = self.rsem.at[plane, (dz + NZ - shift) % NZ, part]
             push(view, view, self.ssem.at[self.count], rsem, dev)
@@ -166,46 +167,42 @@
                 self.send(plane, 0, "d", 1 - part)
 
         def hop(self, plane, dist):
-            near = NZ // 2 if plane == 0 else self.near
+            end = FAR - 1 if plane == 1 else FAR
             for turn in (0, 1):
                 for dz, way, part in ((NZ - dist, "u", turn), (dist, "d", 1 - turn)):
                     self.wait(plane, dz, part)
-                    if dist < near and (dist < NZ // 2 - 1 or turn == 0):
+                    if dist + 1 < end or dist + 1 == end and turn == 0:
                         self.send(plane, dz, way, part)
+                    if plane == 0 and dist == FAR - 1 and turn == 1:
+                        self.send(plane, dz, "y", part)
             for dz in (NZ - dist, dist):
-                self.out(plane, dz, dist)
-
-        def out(self, plane, dz, dist):
-            if plane == 0 and dist > self.near:
-                self.send(0, dz, "y")
-            self.send(plane, dz, "s")
+                self.send(plane, dz, "s")
 
         def last(self, plane):
-            self.wait(plane, NZ // 2, 0)
-            self.wait(plane, NZ // 2, 1)
-            self.out(plane, NZ // 2, NZ // 2)
+            self.wait(plane, FAR, 0)
+            self.wait(plane, FAR, 1)
+            if plane == 0:
+                self.send(0, FAR, "y")
+            self.send(plane, FAR, "s")
 
     tok = Ring(xg, 2, xs, xr, ((0, HALF), (HALF, XROWS - HALF)))
-    mix = Ring(mx, 1, ms, mr, tuple((BLK * b, BLK) for b in range(NB)))
+    mix = Ring(mx, 1, ms, mr, PIECES)
     win = Column(
         lambda plane, z_, rows: wg.at[((yl + plane) % NY) * NZ + z_, :, rows, :],
-        wsend, wrecv, wsib, NEAR,
+        wsend, wrecv, wsib,
     )
     wout = Column(
-        lambda plane, z_, rows: wo.at[plane, z_, rows, :],
-        osend, orecv, osib, NZ // 2,
-    )
-
-    win.send(0, 0, "y")
+        lambda plane, z_, rows: wo.at[(yl + plane) % NY, z_, rows, :],
+        osend, orecv, osib,
+    )
+
+    tok.send(0, 0, 0, "y")
     win.start(0)
-    for half, way in ((0, "y"), (0, "r"), (1, "l"), (1, "y"), (1, "r"), (0, "l")):
+    for half, way in ((0, "r"), (1, "l"), (1, "y"), (1, "r"), (0, "l")):
         tok.send(0, 0, half, way)
     win.send(0, 0, "s")
     for copy in loads[3:]:
         copy.wait()
-    mine = yo.at[2 * yh + yl]
-    for i, dev in enumerate((beside, across, corner)):
-        push(mine, mine, ys.at[i], yr.at[i], dev)
 
     acc[...] = jnp.zeros_like(acc)
     ss[...] = jnp.zeros_like(ss)
@@ -225,11 +222,12 @@
             ag[2 * slot, rows, :] = a[:, 0:256]
             ag[2 * slot + 1, rows, :] = a[:, 256:512]
 
-    def spread_filters():
-        ext[:, 0:BLK] = filt_v[...].astype(F32)
-        ext[:, BLK:] = jnp.zeros((ext.shape[0], BLK), F32)
-
-        @pl.loop(0, ext.shape[0])
+    def spread_filters(piece):
+        if piece == 0:
+            ext[:, 0:BLK] = filt_v[...].astype(F32)
+            ext[:, BLK:] = jnp.zeros((ext.shape[0], BLK), F32)
+
+        @pl.loop(8 * piece, 8 * piece + 8)
         def _(g):
             row_ = jnp.broadcast_to(ext[pl.ds(g, 1), :], (2 * BLK, 2 * BLK))
             shifted = pltpu.roll(row_, BLK, 1, stride=1, stride_axis=0)
@@ -238,7 +236,9 @@
     opposite = tok.slot(0, 2)
     opposite_there = tok.slot(1, 2)
 
-    def project(count, q_of, when):
+    def project(count, q_of, when, begin=0, size=ROWS):
+        rows = slice(begin, begin + size)
+
         @pl.loop(0, count)
         def _(k):
             q = q_of(k)
@@ -247,78 +247,136 @@
             def _():
                 @pl.loop(0, 3)
                 def _(s):
-                    acc[s, 8 : 8 + ROWS, :] += jnp.dot(ag[q], wg[q, s], preferred_element_type=F32)
+                    acc[s, 8 + begin : 8 + begin + size, :] += jnp.dot(
+                        ag[q, rows], wg[q, s], preferred_element_type=F32
+                    )
+
+    def project_pair(count, slot_of, when, begin=0, size=ROWS):
+        rows = slice(begin, begin + size)
+
+        @pl.loop(0, count)
+        def _(k):
+            q = 2 * slot_of(k)
+
+            @pl.when(when(slot_of(k)))
+            def _():
+                a = jnp.concatenate([ag[q, rows], ag[q + 1, rows]], axis=1)
+
+                @pl.loop(0, 3)
+                def _(s):
+                    w = jnp.concatenate([wg[q, s], wg[q + 1, s]], axis=0)
+                    acc[s, 8 + begin : 8 + begin + size, :] += jnp.dot(a, w, preferred_element_type=F32)
 
     norm(0, 0)
     win.hop(0, 1)
-    win.wait(1, 0)
-    win.send(1, 0, "s")
-    spread_filters()
-    win.hop(0, 2)
+    win.send(0, 0, "y")
     tok.wait(1, 0, 0)
     tok.send(1, 0, 0, "r")
+    tok.send(1, 0, 0, "l")
+    spread_filters(0)
+    win.hop(0, 2)
     tok.wait(1, 0, 1)
     tok.send(1, 0, 1, "l")
     tok.send(1, 0, 1, "r")
-    tok.send(1, 0, 0, "l")
-    win.hop(0, 3)
-    win.start(1)
+    push(yo.at[0], yo.at[1], ys.at[0], yr.at[0], corner)
     for dx in (NX - 1, 1):
         tok.wait(0, dx, 0)
         tok.wait(0, dx, 1)
         norm(0, dx)
     norm(1, 0)
-    win.last(0)
+    spread_filters(1)
+    win.hop(0, 3)
+    win.wait(1, 0)
+    win.start(1)
+    win.send(1, 0, "s")
     tok.wait(1, NX - 1, 0)
     tok.send(1, NX - 1, 0, "r")
+    tok.send(0, NX - 1, 0, "r")
+    spread_filters(2)
+    win.last(0)
+    for dz in range(NZ):
+        win.wait_sib(0, dz)
+    beyond = [tok.slot(1, NX - 1), tok.slot(1, 1)]
+
+    def early(slot):
+        ok = jnp.logical_and(slot != opposite, slot != opposite_there)
+        return jnp.logical_and(ok, jnp.logical_and(slot != beyond[0], slot != beyond[1]))
+
+    project_pair(4, lambda k: yl * (NZ // 2) + k, early)
+    tok.wait(1, 1, 0)
     tok.wait(1, 1, 1)
     tok.send(1, 1, 1, "l")
-    for i, (l_, h_) in enumerate(((1 - yl, yh), (yl, 1 - yh), (1 - yl, 1 - yh))):
-        arrived(yo.at[2 * h_ + l_], ys.at[i], yr.at[i])
-    for plane in range(NY):
-        wo[plane, z, my_rows, :] = yo[2 * plane + yh]
+    tok.send(0, 1, 1, "l")
     win.hop(1, 1)
-    tok.send(0, NX - 1, 0, "r")
-    tok.send(0, 1, 1, "l")
-    for plane in range(NY):
-        wout.start(plane)
-        wout.send(plane, 0, "s")
+    norm(1, 1)
     tok.wait(1, NX - 1, 1)
     norm(1, NX - 1)
-    tok.wait(1, 1, 0)
-    norm(1, 1)
-    for dz in range(NZ):
-        win.wait_sib(0, dz)
+    arrived(yo.at[1], ys.at[0], yr.at[0])
+    wo[yl, z, my_rows, :] = jnp.where(yl == yh, yo[0], yo[1])
+    wout.send(0, 0, "y")
+    spread_filters(3)
+    project_pair(2, lambda k: (1 - yh) * NX + (x + 1 + 2 * k) % NX, lambda slot: yh != yl)
+    for dz in (0, 1, 7):
+        win.wait_sib(1, dz)
+
+    def there(k):
+        return (1 - yl) * NZ + (z + NZ - 1 + k) % NZ
+
     project(
-        8, lambda k: yl * NZ + k,
-        lambda q: jnp.logical_and(q // 2 != opposite, q // 2 != opposite_there),
-    )
-    for dz in (5, 3):
-        win.wait(1, dz)
-        win.send(1, dz, "s")
+        3, there, lambda q: jnp.logical_and(q // 2 != opposite, q // 2 != opposite_there)
+    )
     win.hop(1, 2)
-    for plane in range(NY):
-        wout.hop(plane, 1)
+    wout.start(0)
+    wout.send(0, 0, "s")
     tok.wait(1, 2, 0)
     tok.wait(1, 2, 1)
     norm(1, 2)
-    project(2, lambda k: 2 * opposite_there + k, lambda q: yh != yl)
-    for dz in (0, 1, 7, 2, 6, 5, 3):
-        win.wait_sib(1, dz)
+    project_pair(1, lambda k: opposite_there, lambda slot: yh != yl)
     project(
-        7, lambda k: (1 - yl) * NZ + (z + k + (k > 3).astype(jnp.int32)) % NZ,
-        lambda q: q // 2 != opposite,
-    )
-    win.wait(1, 4)
-    win.send(1, 4, "s")
+        3, there, lambda q: jnp.logical_and(q // 2 == opposite_there, yh == yl)
+    )
+    win.wait(1, FAR)
+    win.send(1, FAR, "s")
+    win.wait_sib(1, 2)
+    win.wait_sib(1, 6)
+    project(
+        2, lambda k: (1 - yl) * NZ + (z + 2 + 4 * k) % NZ, lambda q: q // 2 != opposite
+    )
+    wout.wait(1, 0)
+    wout.start(1)
+    wout.send(1, 0, "s")
+    for dz in (5, 3):
+        win.wait(1, dz, 0)
+        win.wait(1, dz, 1)
+        win.send(1, dz, "s")
+    win.wait_sib(1, FAR)
+    project(1, lambda k: (1 - yl) * NZ + (z + FAR) % NZ, lambda q: q // 2 != opposite)
     tok.wait(0, 2, 0)
     tok.wait(0, 2, 1)
     norm(0, 2)
-    project(2, lambda k: 2 * opposite + k, lambda q: q != (1 - yl) * NZ + (z + 4) % NZ)
-    for plane in range(NY):
-        wout.hop(plane, 2)
-    win.wait_sib(1, 4)
-    project(1, lambda k: (1 - yl) * NZ + (z + 4) % NZ, lambda q: q >= 0)
+    win.wait_sib(1, 5)
+    win.wait_sib(1, 3)
+
+    last_up = (1 - yl) * NZ + (z + FAR + 1) % NZ
+    last_down = (1 - yl) * NZ + (z + FAR - 1) % NZ
+
+    def final(begin, size):
+        rows = slice(begin, begin + size)
+        pieces = [ag[2 * opposite, rows], ag[2 * opposite + 1, rows]]
+        for q in (last_up, last_down):
+            a = ag[q, rows]
+            pieces.append(jnp.where(q // 2 != opposite, a, jnp.zeros_like(a)))
+        a = jnp.concatenate(pieces, axis=1)
+        scale = lax.rsqrt(jnp.sum(ss[rows, :], axis=1, keepdims=True) / D + EPS)
+
+        @pl.loop(0, 3)
+        def _(s):
+            w = jnp.concatenate(
+                [wg[2 * opposite, s], wg[2 * opposite + 1, s], wg[last_up, s], wg[last_down, s]], axis=0
+            )
+            there = slice(8 + begin, 8 + begin + size)
+            total = acc[s, there, :] + jnp.dot(a, w, preferred_element_type=F32)
+            acc[s, there, :] = (total * scale).astype(BF).astype(F32)
 
     lanes_group = lax.broadcasted_iota(jnp.int32, (BLK, 128), 1) // GSIZE
 
@@ -329,13 +387,6 @@
         total = total + short_v[1, s : s + 1, cols] * pltpu.roll(v, 1, 0)
         total = total + short_v[2, s : s + 1, cols] * pltpu.roll(v, 2, 0)
         return total[8:]
-
-    def settle(b):
-        rows = pl.ds(pl.multiple_of(b * BLK, BLK), BLK)
-        scale = lax.rsqrt(jnp.sum(ss[rows, :], axis=1, keepdims=True) / D + EPS)
-        at_ = pl.ds(pl.multiple_of(b * BLK + 8, 8), BLK)
-        for s in range(3):
-            acc[s, at_, :] = (acc[s, at_, :] * scale).astype(BF).astype(F32)
 
     def gate(b):
         for j in range(4):
@@ -371,85 +422,97 @@
             acc[s, 0:8, :] = jnp.where(inside, hs_recv[s].astype(F32)[8:16], 0.0)
         gated[0:BLK, :] = jnp.where(inside, gated[0:BLK, :].astype(F32), 0.0).astype(BF)
 
-    def give(b):
-        for way in ("r", "l") if b % 2 else ("l", "r"):
-            mix.send(0, 0, b, way)
-
-    def relay(b):
-        mix.wait(0, NX - 1, b)
-        mix.send(0, NX - 1, b, "r")
-        mix.wait(0, 1, b - 1)
-        mix.send(0, 1, b - 1, "l")
-
-    settle(5)
-    settle(4)
+    def give(c):
+        for piece, way in ((2 * c, "r"), (2 * c + 1, "l"), (2 * c + 1, "r"), (2 * c, "l")):
+            mix.send(0, 0, piece, way)
+
+    def relay(c):
+        mix.wait(0, NX - 1, 2 * c)
+        mix.send(0, NX - 1, 2 * c, "r")
+        mix.wait(0, 1, 2 * c + 1)
+        mix.send(0, 1, 2 * c + 1, "l")
+
+    final(HALF, HALF)
+    wout.hop(0, 1)
     gate(5)
     halo_out()
-    settle(3)
     gate(4)
     combine(5)
-    give(5)
-    settle(2)
+    mix.send(0, 0, 0, "r")
+    mix.send(0, 0, 0, "l")
+    wout.hop(0, 2)
+    final(0, HALF)
     gate(3)
     combine(4)
-    give(4)
-    settle(1)
+    mix.send(0, 0, 1, "l")
+    mix.send(0, 0, 1, "r")
+    wout.hop(0, 3)
+    wout.hop(1, 1)
     gate(2)
     combine(3)
-    settle(0)
     gate(1)
     combine(2)
+    relay(0)
+    give(1)
+    wout.last(0)
     halo_in()
     gate(0)
     combine(1)
     combine(0)
-    relay(5)
+    wout.hop(1, 2)
+    relay(1)
+    give(2)
     give(3)
-    give(2)
-    for plane in range(NY):
-        wout.hop(plane, 3)
-
-    def product(plane, c):
+    for dz in (5, 3):
+        wout.wait(1, dz, 0)
+        wout.wait(1, dz, 1)
+        wout.send(1, dz, "s")
+    wout.wait(1, FAR)
+    wout.send(1, FAR, "s")
+
+    def product(plane, rows):
         total = None
         for x_ in range(NX):
             w = wo[plane, 2 * x_ : 2 * x_ + 2].reshape(COLS, COLS)
-            term = jnp.dot(mx[x_, CHUNK * c : CHUNK * (c + 1), :], w, preferred_element_type=F32)
+            term = jnp.dot(mx[x_, rows, :], w, preferred_element_type=F32)
             total = term if total is None else total + term
         return total
 
-    def outward(c):
-        b = 2 * c + 1
-        for dx, piece in ((NX - 1, b - 1), (1, b), (2, b), (2, b - 1)):
+    def theirs(c):
+        for dx, piece in ((NX - 1, 2 * c + 1), (1, 2 * c), (2, 2 * c), (2, 2 * c + 1)):
             mix.wait(0, dx, piece)
-        rows = slice(CHUNK * c, CHUNK * (c + 1))
-        part_send[rows, :] = product(1 - yh, c).astype(BF)
-        there = pl.ds(CHUNK * c, CHUNK)
+        rows = slice(CHUNKS[c][0], sum(CHUNKS[c]))
+        there = pl.ds(*CHUNKS[c])
+        part_send[rows, :] = product(1 - yh, rows).astype(BF)
         push(part_send.at[there, :], part_recv.at[there, :], ps.at[c], pr.at[c], across)
-        acc2[rows, :] = xg[own, rows, :].astype(F32) + product(yh, c)
+
+    def ours(c):
+        rows = slice(CHUNKS[c][0], sum(CHUNKS[c]))
+        acc2[rows, :] = xg[own, rows, :].astype(F32) + product(yh, rows)
 
     def finish(c):
-        there = pl.ds(CHUNK * c, CHUNK)
-        rows = slice(CHUNK * c, CHUNK * (c + 1))
+        rows = slice(CHUNKS[c][0], sum(CHUNKS[c]))
+        there = pl.ds(*CHUNKS[c])
         arrived(part_recv.at[there, :], ps.at[c], pr.at[c])
         out_v[rows, :] = (acc2[rows, :] + part_recv[rows, :].astype(F32)).astype(BF)
         copy = pltpu.make_async_copy(out_v.at[there, :], out_ref.at[there, :], ls.at[c])
         copy.start()
         return copy
 
+    for plane in range(NY):
+        for dz in range(NZ):
+            wout.wait_sib(plane, dz)
+    theirs(0)
+    relay(2)
+    theirs(1)
     relay(3)
-    give(1)
-    give(0)
-    for plane in range(NY):
-        wout.last(plane)
-    for plane in range(NY):
-        for dz in range(1, NZ):
-            wout.wait_sib(plane, dz)
-        wout.wait_sib(plane, 0)
-    outward(2)
-    relay(1)
-    outward(1)
-    outward(0)
-    stores = [finish(2), finish(1), finish(0)]
+    ours(0)
+    ours(1)
+    theirs(2)
+    theirs(3)
+    ours(2)
+    ours(3)
+    stores = [finish(0), finish(1), finish(2), finish(3)]
     for copy in stores:
         copy.wait()
     for copy in sends:
@@ -469,7 +532,7 @@
             pltpu.VMEM((16, ROWS, 2 * DEPTH), BF),
             pltpu.VMEM((16, 3, 2 * DEPTH, COLS), BF),
             pltpu.VMEM((2, NZ, 2 * DEPTH, COLS), BF),
-            pltpu.VMEM((4, DEPTH, COLS), BF),
+            pltpu.VMEM((2, DEPTH, COLS), BF),
             pltpu.VMEM((4, ROWS, COLS), BF),
             pltpu.VMEM((3, ROWS + 8, COLS), F32),
             pltpu.VMEM((ROWS, COLS), F32),
@@ -488,11 +551,11 @@
             pltpu.VMEM((1, COLS), F32),
             dma((7,)),
             dma((14,)), dma((2, 4, 2)),
-            dma((18,)), dma((1, 4, 6)),
+            dma((24,)), dma((1, 4, 8)),
             dma((50,)), dma((2, 8, 2)), dma((2, 8)),
             dma((60,)), dma((2, 8, 2)), dma((2, 8)),
-            dma((3,)), dma((3,)),
-            dma((3,)), dma((3,)),
+            dma((1,)), dma((1,)),
+            dma((4,)), dma((4,)),
             dma((2,)), dma((2,)),
         ],
         compiler_params=pltpu.CompilerParams(

time: 127 us -> 116 us (0.913); the launches traced: 127 us -> 114 us
  Pallas kernels: 125 us -> 112 us
    pallas_call x1, Pallas kernels: 125 us -> 112 us  [body(): pl.pallas_call(kernel, out_shape=jax.ShapeDtypeStruct((ROWS, COLS), BF),...]
where the time goes in v4:
time: 116 us; the launch traced here: 114 us
  Pallas kernels  112 us (97%)
  local copies, waits for them, and re-layouts  2.06 us (2%)
    pallas_call x1, Pallas kernels, body(): pl.pallas_call(kernel, out_shape=jax.ShapeDtypeStruct((ROWS, COLS), BF),...  112 us

profile of v4, /device:TPU:4, one launch (start us, length us, event | category | flops | bytes accessed | tf_op | source)
XLA Modules:
  0.0 114.0 jit_solution(4147795738738539009)
XLA Ops:
  0.0 112.0 %shard_map.73 = bf16[768,512]{1,0:T(8,128)(2,1)} custom-call(bf16[768,512]{1,0:T(8,128)(2,1)} %tok_ref.1, f32[1,512]{1,0:T(1,128)} %bitcast.6, bf16[3,128,512]{2,1,0:T(8,128)(2,1)} %bitcast.4, f32[3,3,512]{2,1,0:T(4,128)} %short_ref.1, bf16[32,128]{1,0:T(8,128)(2,1)} %bitcast.5, f32[1,512]{1,0:T(1,128)} %bitcast.7, bf16[128,512]{1,0:T(8,128)(2,1)} %outw_ref.1), custom_call_target="tpu_custom_call" | custom-call | tf_op jit(solution)/shard_map/pallas_call | solution.py:525
  112.0 2.1 %copy.9 = bf16[768,512]{1,0:T(8,128)(2,1)} copy(bf16[768,512]{1,0:T(8,128)(2,1)} %shard_map.73) | data formatting | bytes 1572864

commit v5 on v4

--- a/solution.py
+++ b/solution.py
@@ -349,6 +349,7 @@
         win.wait(1, dz, 0)
         win.wait(1, dz, 1)
         win.send(1, dz, "s")
+    wout.hop(0, 1)
     win.wait_sib(1, FAR)
     project(1, lambda k: (1 - yl) * NZ + (z + FAR) % NZ, lambda q: q // 2 != opposite)
     tok.wait(0, 2, 0)
@@ -433,7 +434,6 @@
         mix.send(0, 1, 2 * c + 1, "l")
 
     final(HALF, HALF)
-    wout.hop(0, 1)
     gate(5)
     halo_out()
     gate(4)
@@ -460,15 +460,15 @@
     combine(1)
     combine(0)
     wout.hop(1, 2)
-    relay(1)
-    give(2)
-    give(3)
     for dz in (5, 3):
         wout.wait(1, dz, 0)
         wout.wait(1, dz, 1)
         wout.send(1, dz, "s")
     wout.wait(1, FAR)
     wout.send(1, FAR, "s")
+    relay(1)
+    give(2)
+    give(3)
 
     def product(plane, rows):
         total = None

time: 116 us -> 111 us (0.957); the launches traced: 114 us -> 111 us
  Pallas kernels: 112 us -> 109 us
    pallas_call x1, Pallas kernels: 112 us -> 109 us  [body(): pl.pallas_call(kernel, out_shape=jax.ShapeDtypeStruct((ROWS, COLS), BF),...]
where the time goes in v5:
time: 111 us
  Pallas kernels  109 us (98%)
  local copies, waits for them, and re-layouts  2.06 us (2%)
    pallas_call x1, Pallas kernels, body(): pl.pallas_call(kernel, out_shape=jax.ShapeDtypeStruct((ROWS, COLS), BF),...  109 us

profile of v5, /device:TPU:4, one launch (start us, length us, event | category | flops | bytes accessed | tf_op | source)
XLA Modules:
  0.0 111.3 jit_solution(2190454788545021165)
XLA Ops:
  0.0 109.2 %shard_map.73 = bf16[768,512]{1,0:T(8,128)(2,1)} custom-call(bf16[768,512]{1,0:T(8,128)(2,1)} %tok_ref.1, f32[1,512]{1,0:T(1,128)} %bitcast.6, bf16[3,128,512]{2,1,0:T(8,128)(2,1)} %bitcast.4, f32[3,3,512]{2,1,0:T(4,128)} %short_ref.1, bf16[32,128]{1,0:T(8,128)(2,1)} %bitcast.5, f32[1,512]{1,0:T(1,128)} %bitcast.7, bf16[128,512]{1,0:T(8,128)(2,1)} %outw_ref.1), custom_call_target="tpu_custom_call" | custom-call | tf_op jit(solution)/shard_map/pallas_call | solution.py:525
  109.2 2.1 %copy.9 = bf16[768,512]{1,0:T(8,128)(2,1)} copy(bf16[768,512]{1,0:T(8,128)(2,1)} %shard_map.73) | data formatting | bytes 1572864

commit v6 on v5

--- a/solution.py
+++ b/solution.py
@@ -268,12 +268,13 @@
                     acc[s, 8 + begin : 8 + begin + size, :] += jnp.dot(a, w, preferred_element_type=F32)
 
     norm(0, 0)
+    spread_filters(0)
     win.hop(0, 1)
     win.send(0, 0, "y")
     tok.wait(1, 0, 0)
     tok.send(1, 0, 0, "r")
     tok.send(1, 0, 0, "l")
-    spread_filters(0)
+    spread_filters(1)
     win.hop(0, 2)
     tok.wait(1, 0, 1)
     tok.send(1, 0, 1, "l")
@@ -284,7 +285,7 @@
         tok.wait(0, dx, 1)
         norm(0, dx)
     norm(1, 0)
-    spread_filters(1)
+    spread_filters(2)
     win.hop(0, 3)
     win.wait(1, 0)
     win.start(1)
@@ -292,7 +293,7 @@
     tok.wait(1, NX - 1, 0)
     tok.send(1, NX - 1, 0, "r")
     tok.send(0, NX - 1, 0, "r")
-    spread_filters(2)
+    spread_filters(3)
     win.last(0)
     for dz in range(NZ):
         win.wait_sib(0, dz)
@@ -314,7 +315,6 @@
     arrived(yo.at[1], ys.at[0], yr.at[0])
     wo[yl, z, my_rows, :] = jnp.where(yl == yh, yo[0], yo[1])
     wout.send(0, 0, "y")
-    spread_filters(3)
     project_pair(2, lambda k: (1 - yh) * NX + (x + 1 + 2 * k) % NX, lambda slot: yh != yl)
     for dz in (0, 1, 7):
         win.wait_sib(1, dz)

time: 111 us -> 111 us (level); the launches traced: 111 us -> 110 us
  Pallas kernels: 109 us -> 107 us
    pallas_call x1, Pallas kernels: 109 us -> 107 us  [body(): pl.pallas_call(kernel, out_shape=jax.ShapeDtypeStruct((ROWS, COLS), BF),...]
where the time goes in v6:
time: 111 us; the launch traced here: 110 us
  Pallas kernels  107 us (96%)
  local copies, waits for them, and re-layouts  2.06 us (2%)
    pallas_call x1, Pallas kernels, body(): pl.pallas_call(kernel, out_shape=jax.ShapeDtypeStruct((ROWS, COLS), BF),...  107 us

profile of v6, /device:TPU:4, one launch (start us, length us, event | category | flops | bytes accessed | tf_op | source)
XLA Modules:
  0.0 109.5 jit_solution(6713175096435423223)
XLA Ops:
  0.0 107.4 %shard_map.73 = bf16[768,512]{1,0:T(8,128)(2,1)} custom-call(bf16[768,512]{1,0:T(8,128)(2,1)} %tok_ref.1, f32[1,512]{1,0:T(1,128)} %bitcast.6, bf16[3,128,512]{2,1,0:T(8,128)(2,1)} %bitcast.4, f32[3,3,512]{2,1,0:T(4,128)} %short_ref.1, bf16[32,128]{1,0:T(8,128)(2,1)} %bitcast.5, f32[1,512]{1,0:T(1,128)} %bitcast.7, bf16[128,512]{1,0:T(8,128)(2,1)} %outw_ref.1), custom_call_target="tpu_custom_call" | custom-call | tf_op jit(solution)/shard_map/pallas_call | solution.py:525
  107.4 2.1 %copy.9 = bf16[768,512]{1,0:T(8,128)(2,1)} copy(bf16[768,512]{1,0:T(8,128)(2,1)} %shard_map.73) | data formatting | bytes 1572864
